TPU v7x, 32 devices: a whole 2x2x4 slice. The times are simulated.
32 devices in a mesh: groups: 2 (over y), tm: 8 (over z, x), space: 2 (over core).
Axes of the slice: x: 2, y: 2, z: 4, core: 2. Of those that a mesh axis runs over, the one named last changes fastest.
Arguments:
- interior_diag: bfloat16 [24576, 1536], P(('groups', 'tm'), 'space'), parts along dimension 0, may hold values from -1 to 5, as said below
- coupling: bfloat16 [24576, 1536], P(('groups', 'tm'), 'space'), parts along dimension 0, may hold values from -0.29882812 to 0.29882812
- arrow_rows: bfloat16 [12288, 1536], P(('groups', 'tm', 'space')), parts along dimension 0, may hold values from -0.59765625 to 0.59765625
- separator_diag: bfloat16 [24576, 1536], P(('groups', 'tm'), 'space'), parts along dimension 0, may hold values from -1 to 5, as said below
- tip: bfloat16 [1536, 768], P('groups', 'space'), parts along dimension 0, may hold values from -6 to 6
- lengths: int32 [16], P('groups'), parts along dimension 0, may hold values from 1 to 2, 12 in all
Outputs:
- new_separator: bfloat16 [24576, 1536], P(('groups', 'tm'), 'space'), parts along dimension 0
- arrow_fill: bfloat16 [12288, 1536], P(('groups', 'tm'), 'space'), parts along dimension 0
- new_tip: float32 [1536, 768], P('groups', 'space'), parts along dimension 0
There are 2 independent parts, one for each index of `groups`. A program takes and returns all parts, laid end to end along the dimension named above; each array names one. Nothing has to cross between parts.
Inputs may be any that keep to these rules, and one draw needn't show every extreme that they name: `interior_diag`: each block of 1536 rows is symmetric with eigenvalues above 0.5. `separator_diag`: each block of 1536 rows is symmetric with eigenvalues above 0.5. `lengths`: partition p has an interior block exactly when entry p is 2; some entry is 2.
All inputs are finite; a program needn't handle non-finite values.
Results may differ from a plain program's by a relative error of at most 0.008.
Values may be sent and summed in bfloat16 or wider, within the bound.
No kernel may reach another device: no remote copies, remote signals or barrier semaphores. Data moves between devices by JAX's collectives and lax.ppermute only.
A program may use at most 128 MiB of HBM per device.

v0:
```python
import jax
import jax.numpy as jnp
from jax import lax
from jax.sharding import PartitionSpec as P


def shifted(block, axis, distance):
    devices = range(lax.axis_size(axis))
    route = [(i - distance, i) for i in devices if i - distance in devices]
    return lax.ppermute(block, axis, route)


def solve_block(operands):
    whole_diag, right_sides = operands
    factor = jnp.linalg.cholesky(whole_diag.astype(jnp.float32))
    solved = lax.linalg.triangular_solve(factor, right_sides, left_side=True, lower=True)
    return solved.astype(jnp.bfloat16)


def skip_block(operands):
    return jnp.zeros(operands[1].shape, jnp.bfloat16)


def gram_terms(local_e, local_r, full_e, full_r):
    boundary = jnp.einsum("kb,kc->bc", full_e, local_e, preferred_element_type=jnp.float32)
    arrow_term = -jnp.einsum("ka,kc->ac", full_r, local_e, preferred_element_type=jnp.float32)
    tip_term = jnp.einsum("ka,kc->ac", full_r, local_r, preferred_element_type=jnp.float32)
    return (boundary, arrow_term, tip_term)


def on_device(interior_diag, coupling, arrow_rows, separator_diag, tip, lengths):
    position = lax.axis_index("tm")
    whole_diag = lax.all_gather(interior_diag, "space", axis=1, tiled=True)
    couple = jnp.where(
        position == 0, jnp.zeros(coupling.shape, jnp.float32), coupling.astype(jnp.float32)
    )
    right_sides = jnp.concatenate([couple, arrow_rows.astype(jnp.float32).T], axis=1)
    solved = lax.cond(lengths[position] == 2, solve_block, skip_block, (whole_diag, right_sides))
    split_at = coupling.shape[1]
    solved_e = solved[:, :split_at]
    solved_r = solved[:, split_at:]
    full_e, full_r = (
        lax.all_gather(solved_e, "space", axis=1, tiled=True),
        lax.all_gather(solved_r, "space", axis=1, tiled=True),
    )
    own_boundary, own_arrow, tip_term = gram_terms(solved_e, solved_r, full_e, full_r)
    boundary, arrow_term = (
        shifted(own_boundary.astype(jnp.bfloat16), "tm", -1).astype(own_boundary.dtype),
        shifted(own_arrow.astype(jnp.bfloat16), "tm", -1).astype(own_arrow.dtype),
    )
    tip_sum = lax.psum(tip_term, "tm")
    new_separator = (separator_diag.astype(jnp.float32) - boundary).astype(jnp.bfloat16)
    arrow_fill = arrow_term.astype(jnp.bfloat16)
    new_tip = tip.astype(jnp.float32) - tip_sum
    return (new_separator, arrow_fill, new_tip)


def solution(mesh):
    return jax.shard_map(
        on_device,
        mesh=mesh,
        in_specs=(
            P(("groups", "tm"), "space"),
            P(("groups", "tm"), "space"),
            P(("groups", "tm", "space"), None),
            P(("groups", "tm"), "space"),
            P("groups", "space"),
            P("groups"),
        ),
        out_specs=(
            P(("groups", "tm"), "space"),
            P(("groups", "tm"), "space"),
            P("groups", "space"),
        ),
        check_vma=False,
    )
```

profile of v0, /device:TPU:2, one launch (start us, length us, event | category | flops | bytes accessed | tf_op | source)
XLA Modules:
  0.0 751.8 jit_solution(16959039590199591219)
XLA Ops:
  7.2 0.0 all-gather.4.cloned.1.call-start
  7.2 4.3 copy.10
  11.5 0.0 all-gather.4.cloned.1.call-update
  11.5 0.0 all-gather.6.cloned.1.call-start
  11.6 0.6 dynamic_slice.3
  12.9 1.7 copy.11
  14.6 0.2 convert_bitcast_fusion
  14.7 0.0 copy-done.1
  14.7 0.3 convert_select_fusion
  15.1 3.3 pad_maximum_fusion
  18.4 9.2 %all-gather.4.cloned.1.call-done = bf16[1536,1536]{0,1:T(8,128)(2,1)} async-done(((bf16[1536,768]{0,1:T(8,128)(2,1)}), bf16[1536,1536]{0,1:T(8,128)(2,1)}) %all-gather.4.cloned.1.call-update) | async-done | bytes 4718608 | tf_op jit(solution)/shard_map/all_gather | solution.py:33
  27.6 2.7 conditional.1
  27.6 1.1 slice.446
  28.7 1.6 slice.445
  30.3 0.0 all-gather.6.cloned.1.call-update
  30.3 0.0 all-gather.8.cloned.1.call-start
  30.4 0.7 all-gather.8.cloned.1.call-update
  31.0 0.0 all-reduce.3.cloned.1.call-start
  31.1 580.7 %all-gather.6.cloned.1.call-done = bf16[1536,1536]{1,0:T(8,128)(2,1)} async-done(((bf16[1536,768]{1,0:T(8,128)(2,1)}), bf16[1536,1536]{1,0:T(8,128)(2,1)}) %all-gather.6.cloned.1.call-update) | async-done | bytes 4718608 | tf_op jit(solution)/shard_map/all_gather | solution.py:43
  611.8 8.5 %convolution_convert_fusion.1 = bf16[1536,768]{1,0:T(8,128)(2,1)} fusion(bf16[1536,1536]{1,0:T(8,128)(2,1)} %all-gather.6.cloned.1.call-done, bf16[1536,768]{1,0:T(8,128)(2,1)} %get-tuple-element.20), kind=kOutput, calls=%fused_computation.263 | convolution fusion | flops 3625058304 | bytes 9437184 | tf_op jit(solution)/shard_map/kb,kc->bc/dot_general | solution.py:25
  620.2 2.2 collective-permute-start
  622.4 3.6 all-gather.8.cloned.1.call-done
  626.0 5.6 negate_convert_fusion
  631.6 2.3 collective-permute-start.1
  633.9 3.7 fusion.115
  637.6 0.0 all-reduce.3.cloned.1.call-update
  637.6 83.2 %collective-permute-done.1 = bf16[768,768]{1,0:T(8,128)(2,1)S(1)} collective-permute-done((bf16[768,768]{1,0:T(8,128)(2,1)}, bf16[768,768]{1,0:T(8,128)(2,1)S(1)}, u32[]{:S(2)}, u32[]{:S(2)}) %collective-permute-start.1) | collective-permute-done | bytes 1179680 | tf_op jit(solution)/shard_map/ppermute | solution.py:10
  720.9 17.2 %all-reduce.3.cloned.1.call-done = f32[768,384]{1,0:T(8,128)} async-done(((f32[768,384]{1,0:T(8,128)}), f32[768,384]{1,0:T(8,128)}) %all-reduce.3.cloned.1.call-update) | async-done | bytes 1179664 | tf_op jit(solution)/shard_map/psum | solution.py:51
  738.1 2.5 convert_subtract_fusion
  740.6 0.0 collective-permute-done
  740.6 3.7 subtract_convert_fusion
  744.3 1.0 copy.109
  (7 shorter events, 0.0 us)
Async XLA Ops:
  7.2 4.4 copy-start.6
  7.2 20.4 %all-gather.4.cloned.1.call-start = ((), (), s32[]{:S(2)}) async-start(), calls=%async_computation | async-start | bytes 7077888 | tf_op jit(solution)/shard_map/all_gather | solution.py:33
  11.5 3.2 copy-start.1
  11.5 600.2 %all-gather.6.cloned.1.call-start = ((), (), s32[]{:S(2)}) async-start(), calls=%async_computation.1 | async-start | bytes 7077888 | tf_op jit(solution)/shard_map/all_gather | solution.py:43
  30.3 595.7 %all-gather.8.cloned.1.call-start = ((), (), s32[]{:S(2)}) async-start(), calls=%async_computation.2 | async-start | bytes 3538944 | tf_op jit(solution)/shard_map/all_gather | solution.py:44
  31.0 707.0 %all-reduce.3.cloned.1.call-start = ((), (), s32[]{:S(2)}) async-start(), calls=%async_computation.3 | async-start | bytes 2359296 | tf_op jit(solution)/shard_map/psum | solution.py:51
  620.2 120.4 %collective-permute-start = (bf16[1536,768]{1,0:T(8,128)(2,1)}, bf16[1536,768]{1,0:T(8,128)(2,1)}, u32[]{:S(2)}, u32[]{:S(2)}) collective-permute-start(bf16[1536,768]{1,0:T(8,128)(2,1)} %convolution_convert_fusion.1), channel_id=1, source_target_pairs={{2,0},{4,2},{6,4},{8,6},{10,8},{12,10},{14,12},{3,1},{5,3},{7,5},{... | collective-permute-start | bytes 7077896 | tf_op jit(solution)/shard_map/ppermute | solution.py:10
  626.0 7.9 %copy-start.5 = (bf16[1536,768]{1,0:T(8,128)(2,1)S(1)}, bf16[1536,768]{1,0:T(8,128)(2,1)}, u32[]{:S(2)}) copy-start(bf16[1536,768]{1,0:T(8,128)(2,1)} %all-gather.8.cloned.1.call-done) | copy-start | bytes 7077892
  631.6 109.0 %copy-start.2 = (bf16[1536,768]{1,0:T(8,128)(2,1)S(1)}, bf16[1536,768]{1,0:T(8,128)(2,1)}, u32[]{:S(2)}) copy-start(bf16[1536,768]{1,0:T(8,128)(2,1)} %param.11) | copy-start | bytes 7077892
  631.6 89.3 %collective-permute-start.1 = (bf16[768,768]{1,0:T(8,128)(2,1)}, bf16[768,768]{1,0:T(8,128)(2,1)S(1)}, u32[]{:S(2)}, u32[]{:S(2)}) collective-permute-start(bf16[768,768]{1,0:T(8,128)(2,1)} %negate_convert_fusion), channel_id=1, source_target_pairs={{2,0},{4,2},{6,4},{8,6},{10,8},{12,10},{14,12},{3,1},{5,3},{7,5},{... | collective-permute-start | bytes 3538952 | tf_op jit(solution)/shard_map/ppermute | solution.py:10
Sparse Core Ops, SparseCore 0:
  11.6 15.9 all-gather.3
  30.4 581.2 all-gather.5
  613.9 12.0 all-gather.7
  637.8 100.2 all-reduce.2
where the time goes:
time: 757 us; the launch traced here: 752 us
  waiting for transfers between devices  695 us (92%)
  matrix products  17.7 us (2%)
  between operations  14.5 us (2%)
  local copies, waits for them, and re-layouts  10.3 us (1%)
  other arithmetic  10 us (1%)
    all_gather x1, waiting for transfers between devices, on_device(): lax.all_gather(solved_e, 'space', axis=1, tiled=True)  581 us
    ppermute x2, waiting for transfers between devices, shifted(): return lax.ppermute(block, axis, route)  83.2 us
    psum x1, waiting for transfers between devices, on_device(): tip_sum = lax.psum(tip_term, 'tm')  17.2 us
  transfers between devices with their start and end apart: 6, of which 5 were waited for; matrix products, arithmetic and copies ran while one was open for 4% of the time, Pallas kernels for 0%

commit v1 on v0

v1 whole, which is shorter than its diff:
```python
import functools

import jax
import jax.numpy as jnp
from jax import lax
from jax.experimental import pallas as pl
from jax.experimental.pallas import tpu as pltpu
from jax.sharding import PartitionSpec as P

F32 = jnp.float32
BF16 = jnp.bfloat16
BLOCK = 256
NEAR = 0.03
MOST_STEPS = 60


def shifted(block, axis, distance):
    devices = range(lax.axis_size(axis))
    route = [(i - distance, i) for i in devices if i - distance in devices]
    return lax.ppermute(block, axis, route)


def split(x):
    high = x.astype(BF16)
    return high, (x - high.astype(F32)).astype(BF16)


def nn(a, b):
    return lax.dot_general(a, b, (((1,), (0,)), ((), ())), preferred_element_type=F32)


def nt(a, b):
    return lax.dot_general(a, b, (((1,), (1,)), ((), ())), preferred_element_type=F32)


def three(dot, a, b):
    return dot(a[0], b[0]) + (dot(a[0], b[1]) + dot(a[1], b[0]))


def inverse_root(a, unit_ref, root_ref):
    size = a.shape[0]
    rows = lax.broadcasted_iota(jnp.int32, (size, size), 0)
    columns = lax.broadcasted_iota(jnp.int32, (size, size), 1)
    on_diagonal = rows == columns
    identity = jnp.where(on_diagonal, 1.0, 0.0).astype(F32)
    diagonal = jnp.where(on_diagonal, a, 0.0)
    scale_row = lax.rsqrt(jnp.sum(diagonal, axis=0, keepdims=True))
    scale_column = lax.rsqrt(jnp.sum(diagonal, axis=1, keepdims=True))
    unit = a * scale_row * scale_column
    off = unit - identity
    off_square = nn(off.astype(BF16), off.astype(BF16))
    bound = jnp.sqrt(jnp.sqrt(jnp.sum(off_square * off_square)))
    c = jnp.minimum(1.0, 1.9 / (1.0 + bound))
    gap = c * off - (1.0 - c) * identity
    gap_square = c * c * off_square - (2 * c * (1 - c)) * off + ((1 - c) * (1 - c)) * identity
    first = (jnp.sqrt(c) * (identity - 0.5 * gap + 0.375 * gap_square)).astype(BF16)
    high, low = split(unit)
    product = split(nt(high, first) + nt(low, first))
    gap = nn(first, product[0]) + nn(first, product[1]) - identity
    gap_square = nn(gap.astype(BF16), gap.astype(BF16))
    change = split(0.375 * gap_square - 0.5 * gap)
    root_ref[...] = first.astype(F32) + (nn(change[0], first) + nn(change[1], first))
    unit_ref[...] = unit

    def far(state):
        return jnp.logical_and(state[0] > NEAR**4, state[1] < MOST_STEPS)

    def step(state):
        root = split(root_ref[...])
        product = split(three(nt, split(unit_ref[...]), root))
        gap = three(nn, root, product) - identity
        gap_square = nn(gap.astype(BF16), gap.astype(BF16))
        change = split(0.375 * gap_square - 0.5 * gap)
        root_ref[...] += three(nn, change, root)
        return jnp.sum(gap_square * gap_square), state[1] + 1

    lax.while_loop(far, step, (jnp.sum(gap_square * gap_square), jnp.int32(0)))
    return root_ref[...] * scale_row


def eliminate_kernel(
    flags, diag_ref, e_ref, r_ref, solved_e, solved_r,
    diag, left_e, left_r, high, low, high_t, low_t, unit_ref, root_ref,
):
    size = diag_ref.shape[0]
    block = unit_ref.shape[0]
    steps = size // block

    def at(i):
        return slice(i * block, (i + 1) * block)

    @pl.when(flags[0] == 0)
    def _():
        solved_e[...] = jnp.zeros_like(solved_e)
        solved_r[...] = jnp.zeros_like(solved_r)

    @pl.when(flags[0] != 0)
    def _():
        for i in range(steps):
            diag[at(i), i * block:] = diag_ref[at(i), i * block:].astype(F32)
        left_e[...] = jnp.where(flags[1] != 0, e_ref[...].astype(F32), 0.0)
        left_r[...] = r_ref[...].astype(F32)
        for k in range(steps):
            root = split(inverse_root(diag[at(k), at(k)], unit_ref, root_ref))
            part_e = split(three(nn, root, split(left_e[at(k), :])))
            solved_e[at(k), :] = part_e[0]
            part_r = split(three(nt, split(left_r[:, at(k)]), root))
            solved_r[:, at(k)] = part_r[0]
            for j in range(k + 1, steps):
                panel = three(nn, root, split(diag[at(k), at(j)]))
                high[:, at(j)], low[:, at(j)] = split(panel)
                high_t[at(j), :], low_t[at(j), :] = split(panel.T)
            for i in range(k + 1, steps):
                panel_t = (high_t[at(i), :], low_t[at(i), :])
                for j in range(i, steps):
                    diag[at(i), at(j)] -= three(nn, panel_t, (high[:, at(j)], low[:, at(j)]))
                left_e[at(i), :] -= three(nn, panel_t, part_e)
                left_r[:, at(i)] -= three(nn, part_r, (high[:, at(i)], low[:, at(i)]))


def eliminate(flags, diag, e, r):
    size, block = diag.shape[0], BLOCK
    vmem = pl.BlockSpec(memory_space=pltpu.VMEM)
    return pl.pallas_call(
        eliminate_kernel,
        out_shape=(
            jax.ShapeDtypeStruct(e.shape, BF16),
            jax.ShapeDtypeStruct(r.shape, BF16),
        ),
        in_specs=[pl.BlockSpec(memory_space=pltpu.SMEM), vmem, vmem, vmem],
        out_specs=(vmem, vmem),
        scratch_shapes=[
            pltpu.VMEM((size, size), F32),
            pltpu.VMEM(e.shape, F32),
            pltpu.VMEM(r.shape, F32),
            pltpu.VMEM((block, size), BF16),
            pltpu.VMEM((block, size), BF16),
            pltpu.VMEM((size, block), BF16),
            pltpu.VMEM((size, block), BF16),
            pltpu.VMEM((block, block), F32),
            pltpu.VMEM((block, block), F32),
        ],
        compiler_params=pltpu.CompilerParams(vmem_limit_bytes=58 * 2**20),
    )(flags, diag, e, r)


def gram_terms(local_e, local_r, full_e, full_r):
    boundary = jnp.einsum("kb,kc->bc", full_e, local_e, preferred_element_type=F32)
    arrow_term = -jnp.einsum("ak,kc->ac", full_r, local_e, preferred_element_type=F32)
    tip_term = jnp.einsum("ak,ck->ac", full_r, local_r, preferred_element_type=F32)
    return (boundary, arrow_term, tip_term)


def on_device(interior_diag, coupling, arrow_rows, separator_diag, tip, lengths):
    position = lax.axis_index("tm")
    flags = jnp.stack([lengths[position] == 2, position != 0]).astype(jnp.int32)
    whole_diag = lax.all_gather(interior_diag, "space", axis=1, tiled=True)
    solved_e, solved_r = eliminate(flags, whole_diag, coupling, arrow_rows)
    full_e = lax.all_gather(solved_e, "space", axis=1, tiled=True)
    full_r = lax.all_gather(solved_r, "space", axis=0, tiled=True)
    own_boundary, own_arrow, tip_term = gram_terms(solved_e, solved_r, full_e, full_r)
    boundary = shifted(own_boundary.astype(BF16), "tm", -1).astype(F32)
    arrow_fill = shifted(own_arrow.astype(BF16), "tm", -1)
    tip_sum = lax.psum(tip_term, "tm")
    new_separator = (separator_diag.astype(F32) - boundary).astype(BF16)
    new_tip = tip.astype(F32) - tip_sum
    return (new_separator, arrow_fill, new_tip)


def solution(mesh):
    return jax.shard_map(
        on_device,
        mesh=mesh,
        in_specs=(
            P(("groups", "tm"), "space"),
            P(("groups", "tm"), "space"),
            P(("groups", "tm", "space"), None),
            P(("groups", "tm"), "space"),
            P("groups", "space"),
            P("groups"),
        ),
        out_specs=(
            P(("groups", "tm"), "space"),
            P(("groups", "tm"), "space"),
            P("groups", "space"),
        ),
        check_vma=False,
    )
```

time: 757 us -> 215 us (0.28)
  waiting for transfers between devices: 695 us -> 163 us
    all_gather x2, waiting for transfers between devices: 584 us -> 44.7 us  [the longest x1 40.3 us: on_device(): full_e = lax.all_gather(solved_e, 'space', axis=1, tiled=True)]
  transfers between devices with their start and end apart: 6 -> 6, of which waited for: 5 -> 5; matrix products, arithmetic and copies ran while one was open for 4% -> 9% of each run, Pallas kernels for 0% -> 0%
where the time goes in v1:
time: 215 us; the launch traced here: 212 us
  waiting for transfers between devices  163 us (76%)
  matrix products  14.8 us (7%)
  between operations  14.5 us (7%)
  other arithmetic  6.78 us (3%)
  Pallas kernels  5.58 us (3%)
  starting transfers between devices  4.66 us (2%)
  local copies, waits for them, and re-layouts  2.96 us (1%)
    ppermute x2, waiting for transfers between devices, shifted(): return lax.ppermute(block, axis, route)  84.7 us
    all_gather x1, waiting for transfers between devices, on_device(): full_e = lax.all_gather(solved_e, 'space', axis=1, tiled=True)  40.3 us
    psum x1, waiting for transfers between devices, on_device(): tip_sum = lax.psum(tip_term, 'tm')  16.7 us
    all_gather x1, waiting for transfers between devices, on_device(): whole_diag = lax.all_gather(interior_diag, 'space', axis=1, tiled=True)  15.7 us
    dot_general x1, matrix products, gram_terms(): jnp.einsum('kb,kc->bc', full_e, local_e, preferred_element_type=F32)  7.53 us
    pallas_call x1, Pallas kernels, eliminate(): pl.pallas_call(eliminate_kernel, out_shape=(jax.ShapeDtypeStruct(e.shape,...  5.58 us
    dot_general x1, matrix products, gram_terms(): jnp.einsum('ak,kc->ac', full_r, local_e, preferred_element_type=F32)  4.82 us
    ppermute x2, starting transfers between devices, shifted(): return lax.ppermute(block, axis, route)  4.51 us
  transfers between devices with their start and end apart: 6, of which 5 were waited for; matrix products, arithmetic and copies ran while one was open for 9% of the time, Pallas kernels for 0%

profile of v1, /device:TPU:2, one launch (start us, length us, event | category | flops | bytes accessed | tf_op | source)
XLA Modules:
  0.0 212.4 jit_solution(11356934896295810685)
XLA Ops:
  7.2 0.0 copy-start.4
  7.2 0.0 all-gather.4.cloned.1.call-start
  7.2 0.7 all-gather.4.cloned.1.call-update
  7.9 0.0 all-gather.6.cloned.1.call-start
  8.0 0.0 copy-done.4
  8.0 0.6 dynamic_slice.3
  9.2 0.6 add_convert_fusion.flags
  9.8 15.7 %all-gather.4.cloned.1.call-done.diag_ref = bf16[1536,1536]{1,0:T(8,128)(2,1)} async-done(((bf16[1536,768]{1,0:T(8,128)(2,1)}), bf16[1536,1536]{1,0:T(8,128)(2,1)}) %all-gather.4.cloned.1.call-update) | async-done | bytes 4718608 | tf_op jit(solution)/shard_map/all_gather | solution.py:157
  25.5 5.6 %shard_map.85 = (bf16[1536,768]{1,0:T(8,128)(2,1)}, bf16[384,1536]{1,0:T(8,128)(2,1)}) custom-call(s32[2]{0:T(128)} %add_convert_fusion.flags, bf16[1536,1536]{1,0:T(8,128)(2,1)} %all-gather.4.cloned.1.call-done.diag_ref, bf16[1536,768]{1,0:T(8,128)(2,1)} %e_ref.1, bf16[384,1536]{1,0:T(8,128)(2,1)} %r_ref.1), custom_call_target="tpu_custom_call" | custom-call | tf_op jit(solution)/shard_map/pallas_call | solution.py:124
  31.1 0.0 copy-start.1
  31.1 0.0 all-gather.6.cloned.1.call-update
  31.1 0.0 all-gather.8.cloned.1.call-start
  31.1 0.7 all-gather.8.cloned.1.call-update
  31.8 0.0 all-reduce.2.cloned.1.call-start
  31.9 40.3 %all-gather.6.cloned.1.call-done = bf16[1536,1536]{1,0:T(8,128)(2,1)} async-done(((bf16[1536,768]{1,0:T(8,128)(2,1)}), bf16[1536,1536]{1,0:T(8,128)(2,1)}) %all-gather.6.cloned.1.call-update) | async-done | bytes 4718608 | tf_op jit(solution)/shard_map/all_gather | solution.py:159
  72.2 0.0 copy-done.1
  72.2 7.5 %convolution_convert_fusion = bf16[1536,768]{1,0:T(8,128)(2,1)} fusion(bf16[1536,1536]{1,0:T(8,128)(2,1)} %all-gather.6.cloned.1.call-done, bf16[1536,768]{1,0:T(8,128)(2,1)S(1)} %copy-done.1), kind=kOutput, calls=%fused_computation.1 | convolution fusion | flops 3625058304 | bytes 9437184 | tf_op jit(solution)/shard_map/kb,kc->bc/dot_general | solution.py:148
  79.7 2.3 %collective-permute-start = (bf16[1536,768]{1,0:T(8,128)(2,1)}, bf16[1536,768]{1,0:T(8,128)(2,1)}, u32[]{:S(2)}, u32[]{:S(2)}) collective-permute-start(bf16[1536,768]{1,0:T(8,128)(2,1)} %convolution_convert_fusion), channel_id=1, source_target_pairs={{2,0},{4,2},{6,4},{8,6},{10,8},{12,10},{14,12},{3,1},{5,3},{7,5},{... | collective-permute-start | bytes 7077896 | tf_op jit(solution)/shard_map/ppermute | solution.py:20
  82.1 4.4 %all-gather.8.cloned.1.call-done = bf16[768,1536]{1,0:T(8,128)(2,1)} async-done(((bf16[384,1536]{1,0:T(8,128)(2,1)}), bf16[768,1536]{1,0:T(8,128)(2,1)}) %all-gather.8.cloned.1.call-update) | async-done | bytes 2359312 | tf_op jit(solution)/shard_map/all_gather | solution.py:160
  86.5 4.8 %negate_convert_fusion = bf16[768,768]{1,0:T(8,128)(2,1)} fusion(bf16[768,1536]{1,0:T(8,128)(2,1)} %all-gather.8.cloned.1.call-done, bf16[1536,768]{1,0:T(8,128)(2,1)S(1)} %copy-done.1), kind=kOutput, calls=%fused_computation.2 | convolution fusion | flops 1813118976 | bytes 5898240 | tf_op jit(solution)/shard_map/ak,kc->ac/dot_general | solution.py:149
  91.3 2.2 %collective-permute-start.1 = (bf16[768,768]{1,0:T(8,128)(2,1)}, bf16[768,768]{1,0:T(8,128)(2,1)}, u32[]{:S(2)}, u32[]{:S(2)}) collective-permute-start(bf16[768,768]{1,0:T(8,128)(2,1)} %negate_convert_fusion), channel_id=1, source_target_pairs={{2,0},{4,2},{6,4},{8,6},{10,8},{12,10},{14,12},{3,1},{5,3},{7,5},{... | collective-permute-start | bytes 3538952 | tf_op jit(solution)/shard_map/ppermute | solution.py:20
  93.5 0.0 copy-done.2
  93.5 0.0 copy-done.3
  93.5 2.4 %fusion = f32[768,384]{1,0:T(8,128)} fusion(bf16[768,1536]{1,0:T(8,128)(2,1)S(1)} %copy-done.3, bf16[384,1536]{1,0:T(8,128)(2,1)S(1)} %copy-done.2), kind=kOutput, calls=%fused_computation.5 | convolution fusion | flops 905969664 | bytes 4718592 | tf_op jit(solution)/shard_map/ak,ck->ac/dot_general | solution.py:150
  95.9 0.0 all-reduce.2.cloned.1.call-update
  96.0 84.7 %collective-permute-done.1 = bf16[768,768]{1,0:T(8,128)(2,1)} collective-permute-done((bf16[768,768]{1,0:T(8,128)(2,1)}, bf16[768,768]{1,0:T(8,128)(2,1)}, u32[]{:S(2)}, u32[]{:S(2)}) %collective-permute-start.1) | collective-permute-done | bytes 1179680 | tf_op jit(solution)/shard_map/ppermute | solution.py:20
  180.6 16.7 %all-reduce.2.cloned.1.call-done = f32[768,384]{1,0:T(8,128)} async-done(((f32[768,384]{1,0:T(8,128)}), f32[768,384]{1,0:T(8,128)}) %all-reduce.2.cloned.1.call-update) | async-done | bytes 1179664 | tf_op jit(solution)/shard_map/psum | solution.py:164
  197.4 2.5 %convert_subtract_fusion = f32[768,384]{1,0:T(8,128)} fusion(f32[768,384]{1,0:T(8,128)} %all-reduce.2.cloned.1.call-done, bf16[768,384]{1,0:T(8,128)(2,1)} %param.10), kind=kLoop, calls=%fused_computation.3 | loop fusion | flops 589824 | bytes 2949120 | tf_op jit(solution)/shard_map/sub | solution.py:166
  199.9 0.0 collective-permute-done
  199.9 0.0 copy-done
  199.9 3.7 %subtract_convert_fusion = bf16[1536,768]{1,0:T(8,128)(2,1)} fusion(bf16[1536,768]{1,0:T(8,128)(2,1)} %collective-permute-done, bf16[1536,768]{1,0:T(8,128)(2,1)S(1)} %copy-done), kind=kLoop, calls=%fused_computation | loop fusion | flops 4718592 | bytes 7077888 | tf_op jit(solution)/shard_map/convert_element_type | solution.py:165
  203.5 2.4 %copy.11 = bf16[768,768]{1,0:T(8,128)(2,1)} copy(bf16[768,768]{1,0:T(8,128)(2,1)} %collective-permute-done.1) | data formatting | bytes 2359296
  (3 shorter events, 0.0 us)
Async XLA Ops:
  7.2 0.8 copy-start.4
  7.2 18.3 %all-gather.4.cloned.1.call-start = ((), (), s32[]{:S(2)}) async-start(), calls=%async_computation | async-start | bytes 7077888 | tf_op jit(solution)/shard_map/all_gather | solution.py:157
  7.9 64.3 %all-gather.6.cloned.1.call-start = ((), (), s32[]{:S(2)}) async-start(), calls=%async_computation.1 | async-start | bytes 7077888 | tf_op jit(solution)/shard_map/all_gather | solution.py:159
  31.1 41.1 %copy-start.1 = (bf16[1536,768]{1,0:T(8,128)(2,1)S(1)}, bf16[1536,768]{1,0:T(8,128)(2,1)}, u32[]{:S(2)}) copy-start(bf16[1536,768]{1,0:T(8,128)(2,1)} %get-tuple-element.5) | copy-start | bytes 7077892
  31.1 55.4 %all-gather.8.cloned.1.call-start = ((), (), s32[]{:S(2)}) async-start(), calls=%async_computation.2 | async-start | bytes 3538944 | tf_op jit(solution)/shard_map/all_gather | solution.py:160
  31.8 165.5 %all-reduce.2.cloned.1.call-start = ((), (), s32[]{:S(2)}) async-start(), calls=%async_computation.3 | async-start | bytes 2359296 | tf_op jit(solution)/shard_map/psum | solution.py:164
  79.7 13.8 %copy-start.2 = (bf16[384,1536]{1,0:T(8,128)(2,1)S(1)}, bf16[384,1536]{1,0:T(8,128)(2,1)}, u32[]{:S(2)}) copy-start(bf16[384,1536]{1,0:T(8,128)(2,1)} %get-tuple-element.6) | copy-start | bytes 3538948
  79.7 120.2 %collective-permute-start = (bf16[1536,768]{1,0:T(8,128)(2,1)}, bf16[1536,768]{1,0:T(8,128)(2,1)}, u32[]{:S(2)}, u32[]{:S(2)}) collective-permute-start(bf16[1536,768]{1,0:T(8,128)(2,1)} %convolution_convert_fusion), channel_id=1, source_target_pairs={{2,0},{4,2},{6,4},{8,6},{10,8},{12,10},{14,12},{3,1},{5,3},{7,5},{... | collective-permute-start | bytes 7077896 | tf_op jit(solution)/shard_map/ppermute | solution.py:20
  86.5 7.0 %copy-start.3 = (bf16[768,1536]{1,0:T(8,128)(2,1)S(1)}, bf16[768,1536]{1,0:T(8,128)(2,1)}, u32[]{:S(2)}) copy-start(bf16[768,1536]{1,0:T(8,128)(2,1)} %all-gather.8.cloned.1.call-done) | copy-start | bytes 7077892
  91.3 89.3 %collective-permute-start.1 = (bf16[768,768]{1,0:T(8,128)(2,1)}, bf16[768,768]{1,0:T(8,128)(2,1)}, u32[]{:S(2)}, u32[]{:S(2)}) collective-permute-start(bf16[768,768]{1,0:T(8,128)(2,1)} %negate_convert_fusion), channel_id=1, source_target_pairs={{2,0},{4,2},{6,4},{8,6},{10,8},{12,10},{14,12},{3,1},{5,3},{7,5},{... | collective-permute-start | bytes 3538952 | tf_op jit(solution)/shard_map/ppermute | solution.py:20
  95.9 103.9 %copy-start = (bf16[1536,768]{1,0:T(8,128)(2,1)S(1)}, bf16[1536,768]{1,0:T(8,128)(2,1)}, u32[]{:S(2)}) copy-start(bf16[1536,768]{1,0:T(8,128)(2,1)} %param.9) | copy-start | bytes 7077892
Sparse Core Ops, SparseCore 0:
  9.5 15.9 all-gather.3
  31.2 40.9 all-gather.5
  74.3 12.1 all-gather.7
  96.1 101.2 all-reduce.1

commit v2 on v1

v2 whole, which is shorter than its diff:
```python
import functools

import jax
import jax.numpy as jnp
from jax import lax
from jax.experimental import pallas as pl
from jax.experimental.pallas import tpu as pltpu
from jax.sharding import PartitionSpec as P

F32 = jnp.float32
BF16 = jnp.bfloat16
BLOCK = 256
NEAR = 0.03
MOST_STEPS = 60
STAGES = 7


def split(x):
    high = x.astype(BF16)
    return high, (x - high.astype(F32)).astype(BF16)


def nn(a, b):
    return lax.dot_general(a, b, (((1,), (0,)), ((), ())), preferred_element_type=F32)


def nt(a, b):
    return lax.dot_general(a, b, (((1,), (1,)), ((), ())), preferred_element_type=F32)


def three(dot, a, b):
    return dot(a[0], b[0]) + (dot(a[0], b[1]) + dot(a[1], b[0]))


def total(x):
    return jnp.sum(x, keepdims=True)


def places(size):
    rows = lax.broadcasted_iota(jnp.int32, (size, size), 0)
    columns = lax.broadcasted_iota(jnp.int32, (size, size), 1)
    return rows, columns


def diagonal_row(x, on_diagonal):
    return jnp.sum(jnp.where(on_diagonal, x, 0.0), axis=0, keepdims=True)


def unit_scaled(a, on_diagonal):
    diagonal = jnp.where(on_diagonal, a, 0.0)
    scale_row = lax.rsqrt(jnp.sum(diagonal, axis=0, keepdims=True))
    scale_column = lax.rsqrt(jnp.sum(diagonal, axis=1, keepdims=True))
    return a * scale_row * scale_column, scale_row


def first_root(off, off_square, identity):
    bound = jnp.sqrt(jnp.sqrt(total(off_square * off_square)))
    c = jnp.minimum(1.0, 1.9 / (1.0 + bound))
    gap = c * off - (1.0 - c) * identity
    gap_square = c * c * off_square - (2 * c * (1 - c)) * off + ((1 - c) * (1 - c)) * identity
    return (jnp.sqrt(c) * (identity - 0.5 * gap + 0.375 * gap_square)).astype(BF16)


def root_stages(a, on_diagonal, identity, result):
    unit, scale_row = unit_scaled(a, on_diagonal)
    off = unit - identity
    off_high = off.astype(BF16)
    high, low = split(unit)
    yield
    off_square = nn(off_high, off_high)
    yield
    first = first_root(off, off_square, identity)
    yield
    product = split(nt(high, first) + nt(low, first))
    yield
    gap = nn(first, product[0]) + nn(first, product[1]) - identity
    gap_high = gap.astype(BF16)
    yield
    gap_square = nn(gap_high, gap_high)
    change = split(0.375 * gap_square - 0.5 * gap)
    yield
    root = first.astype(F32) + (nn(change[0], first) + nn(change[1], first))
    result.append(split(root * scale_row))
    result.append(gap_square)


def root_until_near(a, on_diagonal, identity, unit_ref, root_ref):
    unit, scale_row = unit_scaled(a, on_diagonal)
    off = unit - identity
    off_square = nn(off.astype(BF16), off.astype(BF16))
    unit_ref[...] = unit
    root_ref[...] = first_root(off, off_square, identity).astype(F32)

    def far(state):
        return jnp.logical_and(jnp.logical_not(state[0] <= NEAR**4), state[1] < MOST_STEPS)

    def step(state):
        root = split(root_ref[...])
        product = split(three(nt, split(unit_ref[...]), root))
        gap = three(nn, root, product) - identity
        gap_square = nn(gap.astype(BF16), gap.astype(BF16))
        change = split(0.375 * gap_square - 0.5 * gap)
        root_ref[...] += three(nn, change, root)
        return jnp.sum(gap_square * gap_square), state[1] + 1

    lax.while_loop(far, step, (jnp.float32(1.0), jnp.int32(0)))
    return split(root_ref[...] * scale_row)


def interleave(stages, fillers):
    share = -(-len(fillers) // STAGES)
    for _ in stages:
        for filler in fillers[:share]:
            filler()
        fillers = fillers[share:]
    for filler in fillers:
        filler()


def factor_kernel(
    flags, own_d, other_d, r_hbm, out_high, out_low, solved_r,
    given, diag, r_in, left_r, high, low, factor_high, factor_low, near, unit_ref, root_ref, sems,
):
    size, block = diag.shape[0], unit_ref.shape[0]
    half = own_d.shape[1]
    steps = size // block
    core = flags[1]

    def at(i):
        return slice(i * block, (i + 1) * block)

    def arrival(i, which):
        source = own_d if which == 0 else other_d
        side = core if which == 0 else 1 - core
        columns = pl.ds(pl.multiple_of(side * half, half), half)
        return pltpu.make_async_copy(source.at[at(i), :], given.at[at(i), columns], sems.at[which, i])

    def departure(k, which):
        source, target = ((factor_high, out_high), (factor_low, out_low))[which]
        rows = slice(k * block, size)
        return pltpu.make_async_copy(source.at[rows, at(k)], target.at[rows, at(k)], sems.at[2 + which, k])

    rows, columns = places(block)
    on_diagonal = rows == columns
    identity = jnp.where(on_diagonal, 1.0, 0.0).astype(F32)
    r_copy = pltpu.make_async_copy(r_hbm, r_in, sems.at[4, 0])

    @pl.when(flags[0] == 0)
    def _():
        solved_r[...] = jnp.zeros_like(solved_r)

    @pl.when(flags[0] != 0)
    def _():
        for i in range(steps):
            arrival(i, 0).start()
            arrival(i, 1).start()
        r_copy.start()

        def take(i):
            arrival(i, 0).wait()
            arrival(i, 1).wait()
            diag[at(i), i * block:] = given[at(i), i * block:].astype(F32)

        def take_r():
            r_copy.wait()
            left_r[...] = r_in[...].astype(F32)

        take(0)
        result = []
        fillers = [functools.partial(take, i) for i in range(1, steps)] + [take_r]
        interleave(root_stages(diag[at(0), at(0)], on_diagonal, identity, result), fillers)
        for k in range(steps):
            root, gap_square = result
            factor_high[at(k), at(k)], factor_low[at(k), at(k)] = root
            near[k:k + 1, :] = jnp.sum(gap_square * gap_square, axis=0, keepdims=True)
            result, part_r = [], []

            def panel(j):
                value = three(nn, root, split(diag[at(k), at(j)]))
                high[:, at(j)], low[:, at(j)] = split(value)
                factor_high[at(j), at(k)], factor_low[at(j), at(k)] = split(value.T)

            def update(i, j):
                left = (factor_high[at(i), at(k)], factor_low[at(i), at(k)])
                diag[at(i), at(j)] -= three(nn, left, (high[:, at(j)], low[:, at(j)]))

            def solve_r():
                part_r.extend(split(three(nt, split(left_r[:, at(k)]), root)))
                solved_r[:, at(k)] = part_r[0]

            def update_r(i):
                left_r[:, at(i)] -= three(nn, part_r, (high[:, at(i)], low[:, at(i)]))

            fillers = [functools.partial(panel, j) for j in range(k + 2, steps)]
            fillers += [
                functools.partial(update, i, j)
                for i in range(k + 1, steps) for j in range(max(i, k + 2), steps)
            ]
            fillers.append(solve_r)
            fillers += [functools.partial(update_r, i) for i in range(k + 1, steps)]
            if k + 1 < steps:
                panel(k + 1)
                update(k + 1, k + 1)
                stages = root_stages(diag[at(k + 1), at(k + 1)], on_diagonal, identity, result)
                interleave(stages, fillers)
            else:
                interleave((), fillers)
        worst = jnp.max(jnp.sum(near[0:steps, :], axis=1, keepdims=True))

        @pl.when(jnp.logical_not(worst <= NEAR**4))
        def _():
            for i in range(steps):
                diag[at(i), i * block:] = given[at(i), i * block:].astype(F32)
            left_r[...] = r_in[...].astype(F32)

            def spot(i):
                return pl.ds(pl.multiple_of(i * block, block), block)

            def eliminate(k, carry):
                now = spot(k)
                root = root_until_near(diag[now, now], on_diagonal, identity, unit_ref, root_ref)
                factor_high[now, now], factor_low[now, now] = root
                part_r = split(three(nt, split(left_r[:, now]), root))
                solved_r[:, now] = part_r[0]

                def panel(j, carry):
                    there = spot(j)
                    value = three(nn, root, split(diag[now, there]))
                    high[:, there], low[:, there] = split(value)
                    factor_high[there, now], factor_low[there, now] = split(value.T)
                    left_r[:, there] -= three(nn, part_r, (high[:, there], low[:, there]))
                    return carry

                def row(i, carry):
                    here = spot(i)
                    left = (factor_high[here, now], factor_low[here, now])

                    def update(j, carry):
                        there = spot(j)
                        diag[here, there] -= three(nn, left, (high[:, there], low[:, there]))
                        return carry

                    return lax.fori_loop(i, steps, update, carry)

                lax.fori_loop(k + 1, steps, panel, 0)
                lax.fori_loop(k + 1, steps, row, 0)
                return carry

            lax.fori_loop(0, steps, eliminate, 0)

        for k in range(steps):
            departure(k, 0).start()
            departure(k, 1).start()
        for k in range(steps):
            departure(k, 0).wait()
            departure(k, 1).wait()


ANY = pl.BlockSpec(memory_space=pl.ANY)
VMEM = pl.BlockSpec(memory_space=pltpu.VMEM)
SMEM = pl.BlockSpec(memory_space=pltpu.SMEM)


def cost(flops, bytes_accessed):
    return pl.CostEstimate(flops=flops, bytes_accessed=bytes_accessed, transcendentals=0)


def params(mib):
    return pltpu.CompilerParams(vmem_limit_bytes=mib * 2**20)


def factor(flags, own_d, other_d, r):
    size, block = own_d.shape[0], BLOCK
    square = jax.ShapeDtypeStruct((size, size), BF16)
    return pl.pallas_call(
        factor_kernel,
        out_shape=(square, square, jax.ShapeDtypeStruct(r.shape, BF16)),
        in_specs=[SMEM, ANY, ANY, ANY],
        out_specs=(ANY, ANY, VMEM),
        scratch_shapes=[
            pltpu.VMEM((size, size), BF16),
            pltpu.VMEM((size, size), F32),
            pltpu.VMEM(r.shape, BF16),
            pltpu.VMEM(r.shape, F32),
            pltpu.VMEM((block, size), BF16),
            pltpu.VMEM((block, size), BF16),
            pltpu.VMEM((size, size), BF16),
            pltpu.VMEM((size, size), BF16),
            pltpu.VMEM((-(-(size // block) // 8) * 8, block), F32),
            pltpu.VMEM((block, block), F32),
            pltpu.VMEM((block, block), F32),
            pltpu.SemaphoreType.DMA((5, size // block)),
        ],
        compiler_params=params(52),
        cost_estimate=cost(18 * 10**9, 16 * 2**20),
    )(flags, own_d, other_d, r)


def fold(first, second, strict):
    rows, columns = strict
    return jnp.where(rows <= columns, first, second), diagonal_row(second, rows == columns)


def unfold(folded, diagonal, strict):
    rows, columns = strict
    turned = folded.T
    first = jnp.where(rows <= columns, folded, turned)
    second = jnp.where(rows > columns, folded, jnp.where(rows < columns, turned, diagonal))
    return first, second


def solve_kernel(flags, high_hbm, low_hbm, e_ref, solved, packed, high, low, rest, turned, sems):
    size, width = e_ref.shape
    block = BLOCK
    steps = size // block
    half = width // 2

    def at(i):
        return slice(i * block, (i + 1) * block)

    def arrival(j, which):
        source, target = ((high_hbm, high), (low_hbm, low))[which]
        columns = slice(0, (j + 1) * block)
        return pltpu.make_async_copy(source.at[at(j), columns], target.at[at(j), columns], sems.at[which, j])

    @pl.when(flags[2] == 0)
    def _():
        solved[...] = jnp.zeros_like(solved)
        packed[...] = jnp.zeros_like(packed)

    @pl.when(flags[2] != 0)
    def _():
        for j in range(steps):
            arrival(j, 0).start()
            arrival(j, 1).start()
        for j in range(steps):
            arrival(j, 0).wait()
            arrival(j, 1).wait()
            root = (high[at(j), at(j)], low[at(j), at(j)])
            if j == 0:
                part = e_ref[at(j), :]
                value = nn(root[0], part) + nn(root[1], part)
            else:
                before = slice(0, j * block)
                left = (high[at(j), before], low[at(j), before])
                part = e_ref[at(j), :].astype(F32) - three(nn, left, (solved[before, :], rest[before, :]))
                value = three(nn, root, split(part))
            solved[at(j), :], rest[at(j), :] = split(value)
            turned[:, at(j)] = value.T.astype(BF16)
        first = nn(turned[0:half, :], solved[:, 0:half])
        second = nn(turned[half:width, :], solved[:, half:width])
        folded, diagonal = fold(first, second, places(half))
        packed[0:half, :] = folded.astype(BF16)
        packed[half:width, :] = nn(turned[0:half, :], solved[:, half:width]).astype(BF16)
        packed[width:, :] = jnp.broadcast_to(diagonal, (16, half)).astype(BF16)


def solve(flags, high, low, e):
    size, width = e.shape
    return pl.pallas_call(
        solve_kernel,
        out_shape=(
            jax.ShapeDtypeStruct(e.shape, BF16),
            jax.ShapeDtypeStruct((width + 16, width // 2), BF16),
        ),
        in_specs=[SMEM, ANY, ANY, VMEM],
        out_specs=(VMEM, VMEM),
        scratch_shapes=[
            pltpu.VMEM((size, size), BF16),
            pltpu.VMEM((size, size), BF16),
            pltpu.VMEM((size, width), BF16),
            pltpu.VMEM((width, size), BF16),
            pltpu.SemaphoreType.DMA((2, size // BLOCK)),
        ],
        compiler_params=params(40),
        cost_estimate=cost(9 * 10**9, 14 * 2**20),
    )(flags, high, low, e)


def tip_kernel(flags, own_r, other_r, out):
    width = own_r.shape[0]

    @pl.when(flags[0] == 0)
    def _():
        out[...] = jnp.zeros_like(out)

    @pl.when(jnp.logical_and(flags[0] != 0, flags[1] == 0))
    def _():
        out[0:width, :] = nt(own_r[...], other_r[...]).astype(BF16)
        out[width:, :] = jnp.zeros((out.shape[0] - width, width), BF16)

    @pl.when(jnp.logical_and(flags[0] != 0, flags[1] != 0))
    def _():
        first = nt(other_r[...], other_r[...])
        second = nt(own_r[...], own_r[...])
        folded, diagonal = fold(first, second, places(width))
        out[0:width, :] = folded.astype(BF16)
        out[width:, :] = jnp.broadcast_to(diagonal, (out.shape[0] - width, width)).astype(BF16)


def tip_term(flags, own_r, other_r):
    width = own_r.shape[0]
    return pl.pallas_call(
        tip_kernel,
        out_shape=jax.ShapeDtypeStruct((width + 64, width), BF16),
        in_specs=[SMEM, VMEM, VMEM],
        out_specs=VMEM,
        compiler_params=params(16),
        cost_estimate=cost(10**9, 3 * 2**20),
    )(flags, own_r, other_r)


def arrow_kernel(flags, own_r, other_r, own_e, out):
    rows = own_r.shape[0]

    @pl.when(flags[2] == 0)
    def _():
        out[...] = jnp.zeros_like(out)

    @pl.when(flags[2] != 0)
    def _():
        core = flags[1]
        for source, side in ((own_r, core), (other_r, 1 - core)):
            place = pl.ds(pl.multiple_of(side * rows, rows), rows)
            out[place, :] = -nn(source[...], own_e[...]).astype(BF16)


def arrow_term(flags, own_r, other_r, own_e):
    return pl.pallas_call(
        arrow_kernel,
        out_shape=jax.ShapeDtypeStruct((2 * own_r.shape[0], own_e.shape[1]), BF16),
        in_specs=[SMEM, VMEM, VMEM, VMEM],
        out_specs=VMEM,
        compiler_params=params(24),
        cost_estimate=cost(2 * 10**9, 6 * 2**20),
    )(flags, own_r, other_r, own_e)


def cross_kernel(flags, own_e, other_e, out):
    width = own_e.shape[1]
    half = width // 2

    @pl.when(flags[2] == 0)
    def _():
        out[...] = jnp.zeros_like(out)

    @pl.when(jnp.logical_and(flags[2] != 0, flags[1] == 0))
    def _():
        out[...] = nn(other_e[:, 0:half].T, own_e[...]).astype(BF16)

    @pl.when(jnp.logical_and(flags[2] != 0, flags[1] != 0))
    def _():
        out[...] = nn(own_e[:, half:width].T, other_e[...]).astype(BF16)


def cross_term(flags, own_e, other_e):
    width = own_e.shape[1]
    return pl.pallas_call(
        cross_kernel,
        out_shape=jax.ShapeDtypeStruct((width // 2, width), BF16),
        in_specs=[SMEM, VMEM, VMEM],
        out_specs=VMEM,
        compiler_params=params(24),
        cost_estimate=cost(2 * 10**9, 6 * 2**20),
    )(flags, own_e, other_e)


def separator_kernel(flags, separator, packed, own_cross, other_cross, out):
    width = separator.shape[1]
    half = width // 2
    core = flags[1]
    first, second = unfold(
        packed[0:half, :].astype(F32), packed[width:width + 1, :].astype(F32), places(half)
    )
    corner = packed[half:width, :].astype(F32)
    base = pl.multiple_of(core * width, width)

    def less(rows, columns, term):
        out[rows, columns] = (separator[rows, columns].astype(F32) - term).astype(BF16)

    top, bottom = pl.ds(base, half), pl.ds(base + half, half)
    left, right = slice(0, half), slice(half, width)
    less(top, left, first)
    less(top, right, corner)
    less(bottom, left, corner.T)
    less(bottom, right, second)

    @pl.when(core == 0)
    def _():
        less(slice(width, width + half), slice(0, width), own_cross[...].astype(F32))
        less(slice(width + half, 2 * width), slice(0, width), other_cross[...].astype(F32))

    @pl.when(core != 0)
    def _():
        less(slice(0, width), left, other_cross[...].astype(F32).T)
        less(slice(0, width), right, own_cross[...].astype(F32).T)


def separator_less(flags, separator, packed, own_cross, other_cross):
    return pl.pallas_call(
        separator_kernel,
        out_shape=jax.ShapeDtypeStruct(separator.shape, BF16),
        in_specs=[SMEM, VMEM, VMEM, VMEM, VMEM],
        out_specs=VMEM,
        compiler_params=params(24),
        cost_estimate=cost(10**6, 6 * 2**20),
    )(flags, separator, packed, own_cross, other_cross)


def new_tip_kernel(flags, tip, own_sum, other_sum, out):
    width = tip.shape[1]
    core = flags[1]

    @pl.when(core == 0)
    def _():
        first, _ = unfold(
            other_sum[0:width, :].astype(F32), other_sum[width:width + 1, :].astype(F32), places(width)
        )
        out[0:width, :] = tip[0:width, :].astype(F32) - first
        out[width:, :] = tip[width:, :].astype(F32) - own_sum[0:width, :].astype(F32).T

    @pl.when(core != 0)
    def _():
        _, second = unfold(
            own_sum[0:width, :].astype(F32), own_sum[width:width + 1, :].astype(F32), places(width)
        )
        out[0:width, :] = tip[0:width, :].astype(F32) - other_sum[0:width, :].astype(F32)
        out[width:, :] = tip[width:, :].astype(F32) - second


def tip_less(flags, tip, own_sum, other_sum):
    return pl.pallas_call(
        new_tip_kernel,
        out_shape=jax.ShapeDtypeStruct(tip.shape, F32),
        in_specs=[SMEM, VMEM, VMEM, VMEM],
        out_specs=VMEM,
        compiler_params=params(16),
        cost_estimate=cost(10**6, 3 * 2**20),
    )(flags, tip, own_sum, other_sum)


def swapped(x):
    return lax.ppermute(x, "space", [(0, 1), (1, 0)])


def to_previous(x):
    count = lax.axis_size("tm")
    return lax.ppermute(x, "tm", [(i, i - 1) for i in range(1, count)])


def exchanged(x, distance):
    return lax.ppermute(x, "tm", [(i, i ^ distance) for i in range(lax.axis_size("tm"))])


def kept_and_sent(x, upper):
    half = x.shape[0] // 2
    low, high = x[:half], x[half:]
    return jnp.where(upper, high, low), jnp.where(upper, low, high)


def summed(x):
    count = lax.axis_size("tm")
    position = lax.axis_index("tm")
    far = [1 << i for i in range(1, count.bit_length() - 1)]
    halving = far[:2]
    for distance in halving:
        kept, sent = kept_and_sent(x, (position & distance) != 0)
        x = (kept.astype(F32) + exchanged(sent, distance).astype(F32)).astype(BF16)
    for distance in far[2:] + [1]:
        x = (x.astype(F32) + exchanged(x, distance).astype(F32)).astype(BF16)
    for distance in reversed(halving):
        other = exchanged(x, distance)
        upper = (position & distance) != 0
        x = jnp.concatenate([jnp.where(upper, other, x), jnp.where(upper, x, other)], axis=0)
    return x


def on_device(interior_diag, coupling, arrow_rows, separator_diag, tip, lengths):
    position = lax.axis_index("tm")
    active = lengths[position] == 2
    flags = jnp.stack(
        [active, lax.axis_index("space") != 0, jnp.logical_and(active, position != 0)]
    ).astype(jnp.int32)
    other_diag = swapped(interior_diag)
    high, low, own_r = factor(flags, interior_diag, other_diag, arrow_rows)
    other_r = swapped(own_r)
    own_e, packed = solve(flags, high, low, coupling)
    packed = to_previous(packed)
    other_e = swapped(own_e)
    tip_sum = summed(tip_term(flags, own_r, other_r))
    cross = to_previous(cross_term(flags, own_e, other_e))
    arrow_fill = to_previous(arrow_term(flags, own_r, other_r, own_e))
    new_separator = separator_less(flags, separator_diag, packed, cross, swapped(cross))
    new_tip = tip_less(flags, tip, tip_sum, swapped(tip_sum))
    return (new_separator, arrow_fill, new_tip)


def solution(mesh):
    return jax.shard_map(
        on_device,
        mesh=mesh,
        in_specs=(
            P(("groups", "tm"), "space"),
            P(("groups", "tm"), "space"),
            P(("groups", "tm", "space"), None),
            P(("groups", "tm"), "space"),
            P("groups", "space"),
            P("groups"),
        ),
        out_specs=(
            P(("groups", "tm"), "space"),
            P(("groups", "tm"), "space"),
            P("groups", "space"),
        ),
        check_vma=False,
    )
```

time: 215 us -> 135 us (0.63); the launches traced: 212 us -> 135 us
  waiting for transfers between devices: 163 us -> 60.9 us
  Pallas kernels: 5.58 us -> 50.4 us
  matrix products: 14.8 us -> 0 us
  between operations: 14.5 us -> 1.47 us
  starting transfers between devices: 4.66 us -> 14.7 us
  other arithmetic: 6.78 us -> 1.31 us
  local copies, waits for them, and re-layouts: 2.96 us -> 6.01 us
    all_gather x3 -> x0, waiting for transfers between devices: 60.4 us -> none  [the longest x1 40.3 us: on_device(): full_e = lax.all_gather(solved_e, 'space', axis=1, tiled=True)]
    pallas_call x1 -> x7, Pallas kernels: 5.58 us -> 50.4 us  [the longest x1 22.4 us: factor(): pl.pallas_call(factor_kernel, out_shape=(square, square, jax.ShapeDtypeSt...]
    ppermute x2 -> x13, waiting for transfers between devices: 84.7 us -> 60.9 us  [the longest x3 40.5 us: to_previous(): return lax.ppermute(x, 'tm', [(i, i - 1) for i in range(1, count)])]
    psum x1 -> x0, waiting for transfers between devices: 16.7 us -> none  [on_device(): tip_sum = lax.psum(tip_term, 'tm')]
    dot_general x3 -> x0, matrix products: 14.8 us -> none  [the longest x1 7.53 us: gram_terms(): jnp.einsum('kb,kc->bc', full_e, local_e, preferred_element_type=F32)]
    ppermute x2 -> x13, starting transfers between devices: 4.51 us -> 14.7 us  [the longest x3 7.81 us: to_previous(): return lax.ppermute(x, 'tm', [(i, i - 1) for i in range(1, count)])]
    convert_element_type x2 -> x4, other arithmetic: 4.25 us -> 1.13 us  [the longest x2 1.03 us: summed(): x = (kept.astype(F32) + exchanged(sent, distance).astype(F32)).astype(BF16)]
    sub x1 -> x0, other arithmetic: 2.53 us -> none  [on_device(): new_tip = tip.astype(F32) - tip_sum]
  transfers between devices with their start and end apart: 6 -> 13, of which waited for: 5 -> 8; matrix products, arithmetic and copies ran while one was open for 9% -> 2% of each run, Pallas kernels for 0% -> 19%
where the time goes in v2:
time: 135 us
  waiting for transfers between devices  60.9 us (45%)
  Pallas kernels  50.4 us (37%)
  starting transfers between devices  14.7 us (11%)
  local copies, waits for them, and re-layouts  6.01 us (4%)
  between operations  1.47 us (1%)
    ppermute x3, waiting for transfers between devices, to_previous(): return lax.ppermute(x, 'tm', [(i, i - 1) for i in range(1, count)])  40.5 us
    pallas_call x1, Pallas kernels, factor(): pl.pallas_call(factor_kernel, out_shape=(square, square, jax.ShapeDtypeSt...  22.4 us
    ppermute x5, waiting for transfers between devices, exchanged(): lax.ppermute(x, 'tm', [(i, i ^ distance) for i in range(lax.axis_size('tm...  15.8 us
    pallas_call x1, Pallas kernels, solve(): pl.pallas_call(solve_kernel, out_shape=(jax.ShapeDtypeStruct(e.shape, BF1...  14.3 us
    ppermute x3, starting transfers between devices, to_previous(): return lax.ppermute(x, 'tm', [(i, i - 1) for i in range(1, count)])  7.81 us
    ppermute x5, starting transfers between devices, exchanged(): lax.ppermute(x, 'tm', [(i, i ^ distance) for i in range(lax.axis_size('tm...  5.61 us
    unnamed x11, local copies, waits for them, and re-layouts  4.77 us
    ppermute x5, waiting for transfers between devices, swapped(): return lax.ppermute(x, 'space', [(0, 1), (1, 0)])  4.55 us
  transfers between devices with their start and end apart: 13, of which 8 were waited for; matrix products, arithmetic and copies ran while one was open for 2% of the time, Pallas kernels for 19%

profile of v2, /device:TPU:2, one launch (start us, length us, event | category | flops | bytes accessed | tf_op | source)
XLA Modules:
  0.0 134.8 jit_solution(13867436138591369419)
XLA Ops:
  0.6 0.1 collective-permute-start
  0.7 1.2 dynamic_slice.3
  2.6 0.1 add_convert_fusion.3.flags
  2.7 2.7 %collective-permute-done.other_d = bf16[1536,768]{1,0:T(8,128)(2,1)S(1)} collective-permute-done((bf16[1536,768]{1,0:T(8,128)(2,1)}, bf16[1536,768]{1,0:T(8,128)(2,1)S(1)}, u32[]{:S(2)}, u32[]{:S(2)}) %collective-permute-start) | collective-permute-done | bytes 2359328 | tf_op jit(solution)/shard_map/ppermute | solution.py:543
  5.4 1.4 %copy-done.4 = bf16[1536,768]{1,0:T(8,128)(2,1)} copy-done((bf16[1536,768]{1,0:T(8,128)(2,1)}, bf16[1536,768]{1,0:T(8,128)(2,1)S(1)}, u32[]{:S(2)}) %copy-start.4) | copy-done | bytes 2359320
  6.8 22.4 %shard_map.85 = (bf16[1536,1536]{1,0:T(8,128)(2,1)}, bf16[1536,1536]{1,0:T(8,128)(2,1)}, bf16[384,1536]{1,0:T(8,128)(2,1)}) custom-call(s32[3]{0:T(128)S(1)} %add_convert_fusion.3.flags, bf16[1536,768]{1,0:T(8,128)(2,1)} %own_d.1, bf16[1536,768]{1,0:T(8,128)(2,1)} %copy-done.4, bf16[384,1536]{1,0:T(8,128)(2,1)} %r_hbm.1), custom_call_target="tpu_custom_call" | custom-call | flops 17999998976 | bytes 16777216 | tf_op jit(solution)/shard_map/pallas_call | solution.py:275
  29.3 0.2 collective-permute-start.5
  29.5 2.3 %copy-done.3 = bf16[1536,1536]{1,0:T(8,128)(2,1)S(1)} copy-done((bf16[1536,1536]{1,0:T(8,128)(2,1)S(1)}, bf16[1536,1536]{1,0:T(8,128)(2,1)}, u32[]{:S(2)}) %copy-start.3) | copy-done | bytes 4718616
  31.8 14.3 %shard_map.86 = (bf16[1536,768]{1,0:T(8,128)(2,1)S(1)}, bf16[784,384]{1,0:T(8,128)(2,1)S(1)}) custom-call(s32[3]{0:T(128)S(1)} %add_convert_fusion.3.flags, bf16[1536,1536]{1,0:T(8,128)(2,1)S(1)} %copy-done.3, bf16[1536,1536]{1,0:T(8,128)(2,1)} %get-tuple-element.9.low_hbm, bf16[1536,768]{1,0:T(8,128)(2,1)S(1)} %copy-done.2), custom_call_target="tpu_custom_call" | custom-call | flops 8999999488 | bytes 14680064 | tf_op jit(solution)/shard_map/pallas_call | solution.py:360
  46.1 0.4 collective-permute-start.2
  46.6 2.4 %shard_map.90 = bf16[448,384]{1,0:T(8,128)(2,1)S(1)} custom-call(s32[3]{0:T(128)S(1)} %add_convert_fusion.3.flags, bf16[384,1536]{1,0:T(8,128)(2,1)} %get-tuple-element.12.own_r, bf16[384,1536]{1,0:T(8,128)(2,1)} %collective-permute-done.5.other_r), custom_call_target="tpu_custom_call" | custom-call | flops 1000000000 | bytes 3145728 | tf_op jit(solution)/shard_map/pallas_call | solution.py:403
  49.1 7.1 %collective-permute-done.7 = bf16[224,384]{1,0:T(8,128)(2,1)} collective-permute-done((bf16[224,384]{1,0:T(8,128)(2,1)S(1)}, bf16[224,384]{1,0:T(8,128)(2,1)}, u32[]{:S(2)}, u32[]{:S(2)}) %collective-permute-start.7) | collective-permute-done | bytes 172064 | tf_op jit(solution)/shard_map/ppermute | solution.py:552
  56.2 1.0 add_convert_fusion
  57.3 2.7 %collective-permute-start.8 = (bf16[112,384]{1,0:T(8,128)(2,1)S(1)}, bf16[112,384]{1,0:T(8,128)(2,1)S(1)}, u32[]{:S(2)}, u32[]{:S(2)}) collective-permute-start(bf16[112,384]{1,0:T(8,128)(2,1)S(1)} %broadcast_select_fusion.5), channel_id=1, source_target_pairs={{0,8},{2,10},{4,12},{6,14},{8,0},{10,2},{12,4},{14,6},{1,9},{3,11}... | collective-permute-start | bytes 258056 | tf_op jit(solution)/shard_map/ppermute | solution.py:552
  59.9 4.5 %collective-permute-done.8 = bf16[112,384]{1,0:T(8,128)(2,1)S(1)} collective-permute-done((bf16[112,384]{1,0:T(8,128)(2,1)S(1)}, bf16[112,384]{1,0:T(8,128)(2,1)S(1)}, u32[]{:S(2)}, u32[]{:S(2)}) %collective-permute-start.8) | collective-permute-done | bytes 86048 | tf_op jit(solution)/shard_map/ppermute | solution.py:552
  64.5 0.3 collective-permute-start.9
  64.8 4.2 %collective-permute-done.9 = bf16[112,384]{1,0:T(8,128)(2,1)S(1)} collective-permute-done((bf16[112,384]{1,0:T(8,128)(2,1)S(1)}, bf16[112,384]{1,0:T(8,128)(2,1)S(1)}, u32[]{:S(2)}, u32[]{:S(2)}) %collective-permute-start.9) | collective-permute-done | bytes 86048 | tf_op jit(solution)/shard_map/ppermute | solution.py:552
  69.1 0.9 collective-permute-start.10
  70.0 3.1 %shard_map.87 = bf16[384,768]{1,0:T(8,128)(2,1)S(1)} custom-call(s32[3]{0:T(128)S(1)} %add_convert_fusion.3.flags, bf16[1536,768]{1,0:T(8,128)(2,1)S(1)} %get-tuple-element.11.own_e, bf16[1536,768]{1,0:T(8,128)(2,1)} %collective-permute-done.2.other_e), custom_call_target="tpu_custom_call" | custom-call | flops 2000000000 | bytes 6291456 | tf_op jit(solution)/shard_map/pallas_call | solution.py:458
  73.1 1.9 %collective-permute-start.3 = (bf16[384,768]{1,0:T(8,128)(2,1)S(1)}, bf16[384,768]{1,0:T(8,128)(2,1)S(1)}, u32[]{:S(2)}, u32[]{:S(2)}) collective-permute-start(bf16[384,768]{1,0:T(8,128)(2,1)S(1)} %shard_map.87), channel_id=1, source_target_pairs={{2,0},{4,2},{6,4},{8,6},{10,8},{12,10},{14,12},{3,1},{5,3},{7,5},{... | collective-permute-start | bytes 1769480 | tf_op jit(solution)/shard_map/ppermute | solution.py:548
  75.0 3.7 %shard_map.89 = bf16[768,768]{1,0:T(8,128)(2,1)S(1)} custom-call(s32[3]{0:T(128)S(1)} %add_convert_fusion.3.flags, bf16[384,1536]{1,0:T(8,128)(2,1)} %get-tuple-element.12.own_r, bf16[384,1536]{1,0:T(8,128)(2,1)} %collective-permute-done.5.other_r, bf16[1536,768]{1,0:T(8,128)(2,1)S(1)} %get-tuple-element.11.own_e), custom_call_target="tpu_custom_call" | custom-call | flops 2000000000 | bytes 6291456 | tf_op jit(solution)/shard_map/pallas_call | solution.py:429
  78.8 2.1 %collective-permute-start.6 = (bf16[768,768]{1,0:T(8,128)(2,1)S(1)}, bf16[768,768]{1,0:T(8,128)(2,1)S(1)}, u32[]{:S(2)}, u32[]{:S(2)}) collective-permute-start(bf16[768,768]{1,0:T(8,128)(2,1)S(1)} %shard_map.89), channel_id=1, source_target_pairs={{2,0},{4,2},{6,4},{8,6},{10,8},{12,10},{14,12},{3,1},{5,3},{7,5},{... | collective-permute-start | bytes 3538952 | tf_op jit(solution)/shard_map/ppermute | solution.py:548
  80.9 1.6 %collective-permute-start.11 = (bf16[224,384]{1,0:T(8,128)(2,1)S(1)}, bf16[224,384]{1,0:T(8,128)(2,1)S(1)}, u32[]{:S(2)}, u32[]{:S(2)}) collective-permute-start(bf16[224,384]{1,0:T(8,128)(2,1)S(1)} %pad_maximum_fusion.1), channel_id=1, source_target_pairs={{0,4},{2,6},{4,0},{6,2},{8,12},{10,14},{12,8},{14,10},{1,5},{3,7},... | collective-permute-start | bytes 516104 | tf_op jit(solution)/shard_map/ppermute | solution.py:552
  82.5 3.8 %collective-permute-start.1 = (bf16[784,384]{1,0:T(8,128)(2,1)S(1)}, bf16[784,384]{1,0:T(8,128)(2,1)S(1)}, u32[]{:S(2)}, u32[]{:S(2)}) collective-permute-start(bf16[784,384]{1,0:T(8,128)(2,1)S(1)} %get-tuple-element.10), channel_id=1, source_target_pairs={{2,0},{4,2},{6,4},{8,6},{10,8},{12,10},{14,12},{3,1},{5,3},{7,5},{... | collective-permute-start | bytes 1806344 | tf_op jit(solution)/shard_map/ppermute | solution.py:548
  86.3 5.7 %collective-permute-done.3.own_cross = bf16[384,768]{1,0:T(8,128)(2,1)S(1)} collective-permute-done((bf16[384,768]{1,0:T(8,128)(2,1)S(1)}, bf16[384,768]{1,0:T(8,128)(2,1)S(1)}, u32[]{:S(2)}, u32[]{:S(2)}) %collective-permute-start.3) | collective-permute-done | bytes 589856 | tf_op jit(solution)/shard_map/ppermute | solution.py:548
  92.2 0.6 collective-permute-start.12
  92.8 1.8 %collective-permute-done.12.other_sum = bf16[448,384]{1,0:T(8,128)(2,1)S(1)} collective-permute-done((bf16[448,384]{1,0:T(8,128)(2,1)S(1)}, bf16[448,384]{1,0:T(8,128)(2,1)S(1)}, u32[]{:S(2)}, u32[]{:S(2)}) %collective-permute-start.12) | collective-permute-done | bytes 344096 | tf_op jit(solution)/shard_map/ppermute | solution.py:543
  94.6 1.8 %shard_map.91 = f32[768,384]{1,0:T(8,128)} custom-call(s32[3]{0:T(128)S(1)} %add_convert_fusion.3.flags, bf16[768,384]{1,0:T(8,128)(2,1)S(1)} %copy-done.1, bf16[448,384]{1,0:T(8,128)(2,1)S(1)} %pad_maximum_fusion.own_sum, bf16[448,384]{1,0:T(8,128)(2,1)S(1)} %collective-permute-done.12.other_sum), custom_call_target="tpu_custom_call" | custom-call | flops 1000000 | bytes 3145728 | tf_op jit(solution)/shard_map/pallas_call | solution.py:532
  96.4 21.0 %collective-permute-done.6 = bf16[768,768]{1,0:T(8,128)(2,1)S(1)} collective-permute-done((bf16[768,768]{1,0:T(8,128)(2,1)S(1)}, bf16[768,768]{1,0:T(8,128)(2,1)S(1)}, u32[]{:S(2)}, u32[]{:S(2)}) %collective-permute-start.6) | collective-permute-done | bytes 1179680 | tf_op jit(solution)/shard_map/ppermute | solution.py:548
  117.4 13.8 %collective-permute-done.1.packed = bf16[784,384]{1,0:T(8,128)(2,1)S(1)} collective-permute-done((bf16[784,384]{1,0:T(8,128)(2,1)S(1)}, bf16[784,384]{1,0:T(8,128)(2,1)S(1)}, u32[]{:S(2)}, u32[]{:S(2)}) %collective-permute-start.1) | collective-permute-done | bytes 602144 | tf_op jit(solution)/shard_map/ppermute | solution.py:548
  131.2 2.6 %shard_map.88 = bf16[1536,768]{1,0:T(8,128)(2,1)} custom-call(s32[3]{0:T(128)S(1)} %add_convert_fusion.3.flags, bf16[1536,768]{1,0:T(8,128)(2,1)S(1)} %copy-done, bf16[784,384]{1,0:T(8,128)(2,1)S(1)} %collective-permute-done.1.packed, bf16[384,768]{1,0:T(8,128)(2,1)S(1)} %collective-permute-done.3.own_cross, ...), custom_call_target="tpu_custom_call" | custom-call | flops 1000000 | bytes 6291456 | tf_op jit(solution)/shard_map/pallas_call | solution.py:500
  133.8 1.0 copy.10
  (23 shorter events, 0.4 us)
Async XLA Ops:
  0.6 4.8 %collective-permute-start = (bf16[1536,768]{1,0:T(8,128)(2,1)}, bf16[1536,768]{1,0:T(8,128)(2,1)S(1)}, u32[]{:S(2)}, u32[]{:S(2)}) collective-permute-start(bf16[1536,768]{1,0:T(8,128)(2,1)} %own_d.1), channel_id=1, source_target_pairs={{0,1},{1,0},{2,3},{3,2},{4,5},{5,4},{6,7},{7,6},{8,9},{9,8},{10,11... | collective-permute-start | bytes 7077896 | tf_op jit(solution)/shard_map/ppermute | solution.py:543
  2.7 26.8 %copy-start.2 = (bf16[1536,768]{1,0:T(8,128)(2,1)S(1)}, bf16[1536,768]{1,0:T(8,128)(2,1)}, u32[]{:S(2)}) copy-start(bf16[1536,768]{1,0:T(8,128)(2,1)} %e_ref.1) | copy-start | bytes 7077892
  5.4 1.4 %copy-start.4 = (bf16[1536,768]{1,0:T(8,128)(2,1)}, bf16[1536,768]{1,0:T(8,128)(2,1)S(1)}, u32[]{:S(2)}) copy-start(bf16[1536,768]{1,0:T(8,128)(2,1)S(1)} %collective-permute-done.other_d) | copy-start | bytes 7077892
  29.3 17.3 %collective-permute-start.5 = (bf16[384,1536]{1,0:T(8,128)(2,1)}, bf16[384,1536]{1,0:T(8,128)(2,1)}, u32[]{:S(2)}, u32[]{:S(2)}) collective-permute-start(bf16[384,1536]{1,0:T(8,128)(2,1)} %get-tuple-element.12.own_r), channel_id=1, source_target_pairs={{0,1},{1,0},{2,3},{3,2},{4,5},{5,4},{6,7},{7,6},{8,9},{9,8},{10,11... | collective-permute-start | bytes 3538952 | tf_op jit(solution)/shard_map/ppermute | solution.py:543
  29.5 2.3 %copy-start.3 = (bf16[1536,1536]{1,0:T(8,128)(2,1)S(1)}, bf16[1536,1536]{1,0:T(8,128)(2,1)}, u32[]{:S(2)}) copy-start(bf16[1536,1536]{1,0:T(8,128)(2,1)} %get-tuple-element.8.high_hbm) | copy-start | bytes 14155780
  46.1 23.9 %collective-permute-start.2 = (bf16[1536,768]{1,0:T(8,128)(2,1)S(1)}, bf16[1536,768]{1,0:T(8,128)(2,1)}, u32[]{:S(2)}, u32[]{:S(2)}) collective-permute-start(bf16[1536,768]{1,0:T(8,128)(2,1)S(1)} %get-tuple-element.11.own_e), channel_id=1, source_target_pairs={{0,1},{1,0},{2,3},{3,2},{4,5},{5,4},{6,7},{7,6},{8,9},{9,8},{10,11... | collective-permute-start | bytes 7077896 | tf_op jit(solution)/shard_map/ppermute | solution.py:543
  49.0 7.2 %collective-permute-start.7 = (bf16[224,384]{1,0:T(8,128)(2,1)S(1)}, bf16[224,384]{1,0:T(8,128)(2,1)}, u32[]{:S(2)}, u32[]{:S(2)}) collective-permute-start(bf16[224,384]{1,0:T(8,128)(2,1)S(1)} %broadcast_select_fusion.2), channel_id=1, source_target_pairs={{0,4},{2,6},{4,0},{6,2},{8,12},{10,14},{12,8},{14,10},{1,5},{3,7},... | collective-permute-start | bytes 516104 | tf_op jit(solution)/shard_map/ppermute | solution.py:552
  57.3 7.2 %collective-permute-start.8 = (bf16[112,384]{1,0:T(8,128)(2,1)S(1)}, bf16[112,384]{1,0:T(8,128)(2,1)S(1)}, u32[]{:S(2)}, u32[]{:S(2)}) collective-permute-start(bf16[112,384]{1,0:T(8,128)(2,1)S(1)} %broadcast_select_fusion.5), channel_id=1, source_target_pairs={{0,8},{2,10},{4,12},{6,14},{8,0},{10,2},{12,4},{14,6},{1,9},{3,11}... | collective-permute-start | bytes 258056 | tf_op jit(solution)/shard_map/ppermute | solution.py:552
  64.5 4.6 %collective-permute-start.9 = (bf16[112,384]{1,0:T(8,128)(2,1)S(1)}, bf16[112,384]{1,0:T(8,128)(2,1)S(1)}, u32[]{:S(2)}, u32[]{:S(2)}) collective-permute-start(bf16[112,384]{1,0:T(8,128)(2,1)S(1)} %add_convert_fusion.2), channel_id=1, source_target_pairs={{0,2},{2,0},{4,6},{6,4},{8,10},{10,8},{12,14},{14,12},{1,3},{3,1},... | collective-permute-start | bytes 258056 | tf_op jit(solution)/shard_map/ppermute | solution.py:552
  69.1 11.8 %collective-permute-start.10 = (bf16[112,384]{1,0:T(8,128)(2,1)S(1)}, bf16[112,384]{1,0:T(8,128)(2,1)S(1)}, u32[]{:S(2)}, u32[]{:S(2)}) collective-permute-start(bf16[112,384]{1,0:T(8,128)(2,1)S(1)} %add_convert_fusion.1), channel_id=1, source_target_pairs={{0,8},{2,10},{4,12},{6,14},{8,0},{10,2},{12,4},{14,6},{1,9},{3,11}... | collective-permute-start | bytes 258056 | tf_op jit(solution)/shard_map/ppermute | solution.py:552
  73.1 19.0 %collective-permute-start.3 = (bf16[384,768]{1,0:T(8,128)(2,1)S(1)}, bf16[384,768]{1,0:T(8,128)(2,1)S(1)}, u32[]{:S(2)}, u32[]{:S(2)}) collective-permute-start(bf16[384,768]{1,0:T(8,128)(2,1)S(1)} %shard_map.87), channel_id=1, source_target_pairs={{2,0},{4,2},{6,4},{8,6},{10,8},{12,10},{14,12},{3,1},{5,3},{7,5},{... | collective-permute-start | bytes 1769480 | tf_op jit(solution)/shard_map/ppermute | solution.py:548
  75.0 19.6 %copy-start.1 = (bf16[768,384]{1,0:T(8,128)(2,1)S(1)}, bf16[768,384]{1,0:T(8,128)(2,1)}, u32[]{:S(2)}) copy-start(bf16[768,384]{1,0:T(8,128)(2,1)} %tip.1) | copy-start | bytes 1769476
  78.8 52.4 %copy-start = (bf16[1536,768]{1,0:T(8,128)(2,1)S(1)}, bf16[1536,768]{1,0:T(8,128)(2,1)}, u32[]{:S(2)}) copy-start(bf16[1536,768]{1,0:T(8,128)(2,1)} %separator.1) | copy-start | bytes 7077892
  78.8 38.6 %collective-permute-start.6 = (bf16[768,768]{1,0:T(8,128)(2,1)S(1)}, bf16[768,768]{1,0:T(8,128)(2,1)S(1)}, u32[]{:S(2)}, u32[]{:S(2)}) collective-permute-start(bf16[768,768]{1,0:T(8,128)(2,1)S(1)} %shard_map.89), channel_id=1, source_target_pairs={{2,0},{4,2},{6,4},{8,6},{10,8},{12,10},{14,12},{3,1},{5,3},{7,5},{... | collective-permute-start | bytes 3538952 | tf_op jit(solution)/shard_map/ppermute | solution.py:548
  80.9 11.2 %collective-permute-start.11 = (bf16[224,384]{1,0:T(8,128)(2,1)S(1)}, bf16[224,384]{1,0:T(8,128)(2,1)S(1)}, u32[]{:S(2)}, u32[]{:S(2)}) collective-permute-start(bf16[224,384]{1,0:T(8,128)(2,1)S(1)} %pad_maximum_fusion.1), channel_id=1, source_target_pairs={{0,4},{2,6},{4,0},{6,2},{8,12},{10,14},{12,8},{14,10},{1,5},{3,7},... | collective-permute-start | bytes 516104 | tf_op jit(solution)/shard_map/ppermute | solution.py:552
  82.5 48.7 %collective-permute-start.1 = (bf16[784,384]{1,0:T(8,128)(2,1)S(1)}, bf16[784,384]{1,0:T(8,128)(2,1)S(1)}, u32[]{:S(2)}, u32[]{:S(2)}) collective-permute-start(bf16[784,384]{1,0:T(8,128)(2,1)S(1)} %get-tuple-element.10), channel_id=1, source_target_pairs={{2,0},{4,2},{6,4},{8,6},{10,8},{12,10},{14,12},{3,1},{5,3},{7,5},{... | collective-permute-start | bytes 1806344 | tf_op jit(solution)/shard_map/ppermute | solution.py:548
  92.1 39.1 %collective-permute-start.4 = (bf16[384,768]{1,0:T(8,128)(2,1)S(1)}, bf16[384,768]{1,0:T(8,128)(2,1)S(1)}, u32[]{:S(2)}, u32[]{:S(2)}) collective-permute-start(bf16[384,768]{1,0:T(8,128)(2,1)S(1)} %collective-permute-done.3.own_cross), channel_id=1, source_target_pairs={{0,1},{1,0},{2,3},{3,2},{4,5},{5,4},{6,7},{7,6},{8,9},{9,8},{10,11... | collective-permute-start | bytes 1769480 | tf_op jit(solution)/shard_map/ppermute | solution.py:543
  92.2 2.4 %collective-permute-start.12 = (bf16[448,384]{1,0:T(8,128)(2,1)S(1)}, bf16[448,384]{1,0:T(8,128)(2,1)S(1)}, u32[]{:S(2)}, u32[]{:S(2)}) collective-permute-start(bf16[448,384]{1,0:T(8,128)(2,1)S(1)} %pad_maximum_fusion.own_sum), channel_id=1, source_target_pairs={{0,1},{1,0},{2,3},{3,2},{4,5},{5,4},{6,7},{7,6},{8,9},{9,8},{10,11... | collective-permute-start | bytes 1032200 | tf_op jit(solution)/shard_map/ppermute | solution.py:543

commit v3 on v2

--- a/solution.py
+++ b/solution.py
@@ -117,12 +117,13 @@
         filler()
 
 
-def factor_kernel(
-    flags, own_d, other_d, r_hbm, out_high, out_low, solved_r,
-    given, diag, r_in, left_r, high, low, factor_high, factor_low, near, unit_ref, root_ref, sems,
+def eliminate_kernel(
+    flags, own_d, other_d, e_hbm, r_hbm, solved_e, solved_r, packed,
+    given, diag, e_in, r_in, left_r, high, low, factor_high, factor_low, rest_e, turned,
+    near, unit_ref, root_ref, sems,
 ):
     size, block = diag.shape[0], unit_ref.shape[0]
-    half = own_d.shape[1]
+    half, width = own_d.shape[1], e_in.shape[1]
     steps = size // block
     core = flags[1]
 
@@ -135,19 +136,29 @@
         columns = pl.ds(pl.multiple_of(side * half, half), half)
         return pltpu.make_async_copy(source.at[at(i), :], given.at[at(i), columns], sems.at[which, i])
 
-    def departure(k, which):
-        source, target = ((factor_high, out_high), (factor_low, out_low))[which]
-        rows = slice(k * block, size)
-        return pltpu.make_async_copy(source.at[rows, at(k)], target.at[rows, at(k)], sems.at[2 + which, k])
-
     rows, columns = places(block)
     on_diagonal = rows == columns
     identity = jnp.where(on_diagonal, 1.0, 0.0).astype(F32)
-    r_copy = pltpu.make_async_copy(r_hbm, r_in, sems.at[4, 0])
+    e_copy = pltpu.make_async_copy(e_hbm, e_in, sems.at[2, 0])
+    r_copy = pltpu.make_async_copy(r_hbm, r_in, sems.at[2, 1])
+
+    def solve_e(k, root):
+        part = e_in[at(k), :]
+        if k == 0:
+            value = nn(root[0], part) + nn(root[1], part)
+        else:
+            before = slice(0, k * block)
+            left = (factor_high[at(k), before], factor_low[at(k), before])
+            part = part.astype(F32) - three(nn, left, (solved_e[before, :], rest_e[before, :]))
+            value = three(nn, root, split(part))
+        solved_e[at(k), :], rest_e[at(k), :] = split(value)
+        turned[:, at(k)] = value.T.astype(BF16)
 
     @pl.when(flags[0] == 0)
     def _():
+        solved_e[...] = jnp.zeros_like(solved_e)
         solved_r[...] = jnp.zeros_like(solved_r)
+        packed[...] = jnp.zeros_like(packed)
 
     @pl.when(flags[0] != 0)
     def _():
@@ -155,6 +166,7 @@
             arrival(i, 0).start()
             arrival(i, 1).start()
         r_copy.start()
+        e_copy.start()
 
         def take(i):
             arrival(i, 0).wait()
@@ -167,11 +179,10 @@
 
         take(0)
         result = []
-        fillers = [functools.partial(take, i) for i in range(1, steps)] + [take_r]
+        fillers = [functools.partial(take, i) for i in range(1, steps)] + [take_r, e_copy.wait]
         interleave(root_stages(diag[at(0), at(0)], on_diagonal, identity, result), fillers)
         for k in range(steps):
             root, gap_square = result
-            factor_high[at(k), at(k)], factor_low[at(k), at(k)] = root
             near[k:k + 1, :] = jnp.sum(gap_square * gap_square, axis=0, keepdims=True)
             result, part_r = [], []
 
@@ -198,6 +209,7 @@
             ]
             fillers.append(solve_r)
             fillers += [functools.partial(update_r, i) for i in range(k + 1, steps)]
+            fillers.append(functools.partial(solve_e, k, root))
             if k + 1 < steps:
                 panel(k + 1)
                 update(k + 1, k + 1)
@@ -219,9 +231,18 @@
             def eliminate(k, carry):
                 now = spot(k)
                 root = root_until_near(diag[now, now], on_diagonal, identity, unit_ref, root_ref)
-                factor_high[now, now], factor_low[now, now] = root
                 part_r = split(three(nt, split(left_r[:, now]), root))
                 solved_r[:, now] = part_r[0]
+
+                def left_of(j, part):
+                    there = spot(j)
+                    left = (factor_high[now, there], factor_low[now, there])
+                    return part - three(nn, left, (solved_e[there, :], rest_e[there, :]))
+
+                part_e = lax.fori_loop(0, k, left_of, e_in[now, :].astype(F32))
+                value = three(nn, root, split(part_e))
+                solved_e[now, :], rest_e[now, :] = split(value)
+                turned[:, now] = value.T.astype(BF16)
 
                 def panel(j, carry):
                     there = spot(j)
@@ -248,12 +269,26 @@
 
             lax.fori_loop(0, steps, eliminate, 0)
 
-        for k in range(steps):
-            departure(k, 0).start()
-            departure(k, 1).start()
-        for k in range(steps):
-            departure(k, 0).wait()
-            departure(k, 1).wait()
+        corner = width // 2
+        first = nn(turned[0:corner, :], solved_e[:, 0:corner])
+        second = nn(turned[corner:width, :], solved_e[:, corner:width])
+        folded, diagonal = fold(first, second, places(corner))
+        packed[0:corner, :] = folded.astype(BF16)
+        packed[corner:width, :] = nn(turned[0:corner, :], solved_e[:, corner:width]).astype(BF16)
+        packed[width:, :] = jnp.broadcast_to(diagonal, (16, corner)).astype(BF16)
+
+
+def fold(first, second, strict):
+    rows, columns = strict
+    return jnp.where(rows <= columns, first, second), diagonal_row(second, rows == columns)
+
+
+def unfold(folded, diagonal, strict):
+    rows, columns = strict
+    turned = folded.T
+    first = jnp.where(rows <= columns, folded, turned)
+    second = jnp.where(rows > columns, folded, jnp.where(rows < columns, turned, diagonal))
+    return first, second
 
 
 ANY = pl.BlockSpec(memory_space=pl.ANY)
@@ -269,112 +304,38 @@
     return pltpu.CompilerParams(vmem_limit_bytes=mib * 2**20)
 
 
-def factor(flags, own_d, other_d, r):
+def eliminate(flags, own_d, other_d, e, r):
     size, block = own_d.shape[0], BLOCK
-    square = jax.ShapeDtypeStruct((size, size), BF16)
+    width = e.shape[1]
     return pl.pallas_call(
-        factor_kernel,
-        out_shape=(square, square, jax.ShapeDtypeStruct(r.shape, BF16)),
-        in_specs=[SMEM, ANY, ANY, ANY],
-        out_specs=(ANY, ANY, VMEM),
+        eliminate_kernel,
+        out_shape=(
+            jax.ShapeDtypeStruct(e.shape, BF16),
+            jax.ShapeDtypeStruct(r.shape, BF16),
+            jax.ShapeDtypeStruct((width + 16, width // 2), BF16),
+        ),
+        in_specs=[SMEM, ANY, VMEM, ANY, ANY],
+        out_specs=(VMEM, VMEM, VMEM),
         scratch_shapes=[
             pltpu.VMEM((size, size), BF16),
             pltpu.VMEM((size, size), F32),
+            pltpu.VMEM(e.shape, BF16),
             pltpu.VMEM(r.shape, BF16),
             pltpu.VMEM(r.shape, F32),
             pltpu.VMEM((block, size), BF16),
             pltpu.VMEM((block, size), BF16),
             pltpu.VMEM((size, size), BF16),
             pltpu.VMEM((size, size), BF16),
+            pltpu.VMEM(e.shape, BF16),
+            pltpu.VMEM((width, size), BF16),
             pltpu.VMEM((-(-(size // block) // 8) * 8, block), F32),
             pltpu.VMEM((block, block), F32),
             pltpu.VMEM((block, block), F32),
-            pltpu.SemaphoreType.DMA((5, size // block)),
+            pltpu.SemaphoreType.DMA((3, size // block)),
         ],
         compiler_params=params(52),
-        cost_estimate=cost(18 * 10**9, 16 * 2**20),
-    )(flags, own_d, other_d, r)
-
-
-def fold(first, second, strict):
-    rows, columns = strict
-    return jnp.where(rows <= columns, first, second), diagonal_row(second, rows == columns)
-
-
-def unfold(folded, diagonal, strict):
-    rows, columns = strict
-    turned = folded.T
-    first = jnp.where(rows <= columns, folded, turned)
-    second = jnp.where(rows > columns, folded, jnp.where(rows < columns, turned, diagonal))
-    return first, second
-
-
-def solve_kernel(flags, high_hbm, low_hbm, e_ref, solved, packed, high, low, rest, turned, sems):
-    size, width = e_ref.shape
-    block = BLOCK
-    steps = size // block
-    half = width // 2
-
-    def at(i):
-        return slice(i * block, (i + 1) * block)
-
-    def arrival(j, which):
-        source, target = ((high_hbm, high), (low_hbm, low))[which]
-        columns = slice(0, (j + 1) * block)
-        return pltpu.make_async_copy(source.at[at(j), columns], target.at[at(j), columns], sems.at[which, j])
-
-    @pl.when(flags[2] == 0)
-    def _():
-        solved[...] = jnp.zeros_like(solved)
-        packed[...] = jnp.zeros_like(packed)
-
-    @pl.when(flags[2] != 0)
-    def _():
-        for j in range(steps):
-            arrival(j, 0).start()
-            arrival(j, 1).start()
-        for j in range(steps):
-            arrival(j, 0).wait()
-            arrival(j, 1).wait()
-            root = (high[at(j), at(j)], low[at(j), at(j)])
-            if j == 0:
-                part = e_ref[at(j), :]
-                value = nn(root[0], part) + nn(root[1], part)
-            else:
-                before = slice(0, j * block)
-                left = (high[at(j), before], low[at(j), before])
-                part = e_ref[at(j), :].astype(F32) - three(nn, left, (solved[before, :], rest[before, :]))
-                value = three(nn, root, split(part))
-            solved[at(j), :], rest[at(j), :] = split(value)
-            turned[:, at(j)] = value.T.astype(BF16)
-        first = nn(turned[0:half, :], solved[:, 0:half])
-        second = nn(turned[half:width, :], solved[:, half:width])
-        folded, diagonal = fold(first, second, places(half))
-        packed[0:half, :] = folded.astype(BF16)
-        packed[half:width, :] = nn(turned[0:half, :], solved[:, half:width]).astype(BF16)
-        packed[width:, :] = jnp.broadcast_to(diagonal, (16, half)).astype(BF16)
-
-
-def solve(flags, high, low, e):
-    size, width = e.shape
-    return pl.pallas_call(
-        solve_kernel,
-        out_shape=(
-            jax.ShapeDtypeStruct(e.shape, BF16),
-            jax.ShapeDtypeStruct((width + 16, width // 2), BF16),
-        ),
-        in_specs=[SMEM, ANY, ANY, VMEM],
-        out_specs=(VMEM, VMEM),
-        scratch_shapes=[
-            pltpu.VMEM((size, size), BF16),
-            pltpu.VMEM((size, size), BF16),
-            pltpu.VMEM((size, width), BF16),
-            pltpu.VMEM((width, size), BF16),
-            pltpu.SemaphoreType.DMA((2, size // BLOCK)),
-        ],
-        compiler_params=params(40),
-        cost_estimate=cost(9 * 10**9, 14 * 2**20),
-    )(flags, high, low, e)
+        cost_estimate=cost(28 * 10**9, 16 * 2**20),
+    )(flags, own_d, other_d, e, r)
 
 
 def tip_kernel(flags, own_r, other_r, out):
@@ -582,16 +543,20 @@
         [active, lax.axis_index("space") != 0, jnp.logical_and(active, position != 0)]
     ).astype(jnp.int32)
     other_diag = swapped(interior_diag)
-    high, low, own_r = factor(flags, interior_diag, other_diag, arrow_rows)
-    other_r = swapped(own_r)
-    own_e, packed = solve(flags, high, low, coupling)
+    own_e, own_r, packed = eliminate(flags, interior_diag, other_diag, coupling, arrow_rows)
     packed = to_previous(packed)
     other_e = swapped(own_e)
-    tip_sum = summed(tip_term(flags, own_r, other_r))
-    cross = to_previous(cross_term(flags, own_e, other_e))
-    arrow_fill = to_previous(arrow_term(flags, own_r, other_r, own_e))
-    new_separator = separator_less(flags, separator_diag, packed, cross, swapped(cross))
-    new_tip = tip_less(flags, tip, tip_sum, swapped(tip_sum))
+    other_r = swapped(own_r)
+    cross = cross_term(flags, own_e, other_e)
+    cross = to_previous(cross)
+    arrow = arrow_term(flags, own_r, other_r, own_e)
+    arrow_fill = to_previous(arrow)
+    term = tip_term(flags, own_r, other_r)
+    tip_sum = summed(term)
+    other_cross = swapped(cross)
+    new_separator = separator_less(flags, separator_diag, packed, cross, other_cross)
+    other_sum = swapped(tip_sum)
+    new_tip = tip_less(flags, tip, tip_sum, other_sum)
     return (new_separator, arrow_fill, new_tip)
 
 

time: 135 us -> 129 us (0.956)
  Pallas kernels: 50.4 us -> 13.8 us
  starting transfers between devices: 14.7 us -> 47 us
  local copies, waits for them, and re-layouts: 6.01 us -> 3.68 us
    ppermute x5, starting transfers between devices: 5.61 us -> 39.4 us  [exchanged(): lax.ppermute(x, 'tm', [(i, i ^ distance) for i in range(lax.axis_size('tm...]
    pallas_call x2 -> x1, Pallas kernels: 36.7 us -> 4.16 us  [eliminate(): pl.pallas_call(eliminate_kernel, out_shape=(jax.ShapeDtypeStruct(e.shape,...]
    ppermute x5, waiting for transfers between devices: 4.55 us -> 7.23 us  [swapped(): return lax.ppermute(x, 'space', [(0, 1), (1, 0)])]
    unnamed x11 -> x9, local copies, waits for them, and re-layouts: 4.77 us -> 2.43 us
    pallas_call x1, Pallas kernels: 3.71 us -> 1.79 us  [arrow_term(): pl.pallas_call(arrow_kernel, out_shape=jax.ShapeDtypeStruct((2 * own_r.sh...]
    ppermute x5, waiting for transfers between devices: 15.8 us -> 14 us  [exchanged(): lax.ppermute(x, 'tm', [(i, i ^ distance) for i in range(lax.axis_size('tm...]
    ppermute x3, starting transfers between devices: 7.81 us -> 6.4 us  [to_previous(): return lax.ppermute(x, 'tm', [(i, i - 1) for i in range(1, count)])]
    pallas_call x1, Pallas kernels: 3.09 us -> 1.73 us  [cross_term(): pl.pallas_call(cross_kernel, out_shape=jax.ShapeDtypeStruct((width // 2,...]
  transfers between devices with their start and end apart: 13 -> 13, of which waited for: 8 -> 9; matrix products, arithmetic and copies ran while one was open for 2% -> 2% of each run, Pallas kernels for 19% -> 5%
where the time goes in v3:
time: 129 us
  waiting for transfers between devices  61.9 us (48%)
  starting transfers between devices  47 us (36%)
  Pallas kernels  13.8 us (11%)
  local copies, waits for them, and re-layouts  3.68 us (3%)
  between operations  1.45 us (1%)
  other arithmetic  1.31 us (1%)
    ppermute x3, waiting for transfers between devices, to_previous(): return lax.ppermute(x, 'tm', [(i, i - 1) for i in range(1, count)])  40.6 us
    ppermute x5, starting transfers between devices, exchanged(): lax.ppermute(x, 'tm', [(i, i ^ distance) for i in range(lax.axis_size('tm...  39.4 us
    ppermute x5, waiting for transfers between devices, exchanged(): lax.ppermute(x, 'tm', [(i, i ^ distance) for i in range(lax.axis_size('tm...  14 us
    ppermute x5, waiting for transfers between devices, swapped(): return lax.ppermute(x, 'space', [(0, 1), (1, 0)])  7.23 us
    ppermute x3, starting transfers between devices, to_previous(): return lax.ppermute(x, 'tm', [(i, i - 1) for i in range(1, count)])  6.4 us
    pallas_call x1, Pallas kernels, eliminate(): pl.pallas_call(eliminate_kernel, out_shape=(jax.ShapeDtypeStruct(e.shape,...  4.16 us
    pallas_call x1, Pallas kernels, separator_less(): pl.pallas_call(separator_kernel, out_shape=jax.ShapeDtypeStruct(separator...  2.61 us
  transfers between devices with their start and end apart: 13, of which 9 were waited for; matrix products, arithmetic and copies ran while one was open for 2% of the time, Pallas kernels for 5%

profile of v3, /device:TPU:2, one launch (start us, length us, event | category | flops | bytes accessed | tf_op | source)
XLA Modules:
  0.0 129.1 jit_solution(6653742304102884581)
XLA Ops:
  0.6 0.1 collective-permute-start
  0.7 1.2 dynamic_slice.3
  2.6 0.1 add_convert_fusion.3.flags
  2.7 2.7 %collective-permute-done.other_d = bf16[1536,768]{1,0:T(8,128)(2,1)S(1)} collective-permute-done((bf16[1536,768]{1,0:T(8,128)(2,1)}, bf16[1536,768]{1,0:T(8,128)(2,1)S(1)}, u32[]{:S(2)}, u32[]{:S(2)}) %collective-permute-start) | collective-permute-done | bytes 2359328 | tf_op jit(solution)/shard_map/ppermute | solution.py:504
  5.4 1.4 %copy-done.3 = bf16[1536,768]{1,0:T(8,128)(2,1)} copy-done((bf16[1536,768]{1,0:T(8,128)(2,1)}, bf16[1536,768]{1,0:T(8,128)(2,1)S(1)}, u32[]{:S(2)}) %copy-start.3) | copy-done | bytes 2359320
  6.8 4.2 %shard_map.85 = (bf16[1536,768]{1,0:T(8,128)(2,1)}, bf16[384,1536]{1,0:T(8,128)(2,1)}, bf16[784,384]{1,0:T(8,128)(2,1)S(1)}) custom-call(s32[3]{0:T(128)S(1)} %add_convert_fusion.3.flags, bf16[1536,768]{1,0:T(8,128)(2,1)} %own_d.1, bf16[1536,768]{1,0:T(8,128)(2,1)} %copy-done.3, bf16[1536,768]{1,0:T(8,128)(2,1)} %e_hbm.1, bf16[384,1536]{1,0:T(8,128)(2,1)} %r_hbm.1), custom_call_target="tpu_custom_call" | custom-call | flops 28000000000 | bytes 16777216 | tf_op jit(solution)/shard_map/pallas_call | solution.py:310
  11.0 0.2 collective-permute-start.5
  11.2 0.4 collective-permute-start.2
  11.6 2.7 %collective-permute-done.5.other_r = bf16[384,1536]{1,0:T(8,128)(2,1)} collective-permute-done((bf16[384,1536]{1,0:T(8,128)(2,1)}, bf16[384,1536]{1,0:T(8,128)(2,1)}, u32[]{:S(2)}, u32[]{:S(2)}) %collective-permute-start.5) | collective-permute-done | bytes 1179680 | tf_op jit(solution)/shard_map/ppermute | solution.py:504
  14.3 1.7 %shard_map.89 = bf16[448,384]{1,0:T(8,128)(2,1)S(1)} custom-call(s32[3]{0:T(128)S(1)} %add_convert_fusion.3.flags, bf16[384,1536]{1,0:T(8,128)(2,1)} %get-tuple-element.8.own_r, bf16[384,1536]{1,0:T(8,128)(2,1)} %collective-permute-done.5.other_r), custom_call_target="tpu_custom_call" | custom-call | flops 1000000000 | bytes 3145728 | tf_op jit(solution)/shard_map/pallas_call | solution.py:364
  16.0 29.5 %collective-permute-start.7 = (bf16[224,384]{1,0:T(8,128)(2,1)S(1)}, bf16[224,384]{1,0:T(8,128)(2,1)}, u32[]{:S(2)}, u32[]{:S(2)}) collective-permute-start(bf16[224,384]{1,0:T(8,128)(2,1)S(1)} %broadcast_select_fusion.2), channel_id=1, source_target_pairs={{0,4},{2,6},{4,0},{6,2},{8,12},{10,14},{12,8},{14,10},{1,5},{3,7},... | collective-permute-start | bytes 516104 | tf_op jit(solution)/shard_map/ppermute | solution.py:513
  45.5 5.3 %collective-permute-done.7 = bf16[224,384]{1,0:T(8,128)(2,1)} collective-permute-done((bf16[224,384]{1,0:T(8,128)(2,1)S(1)}, bf16[224,384]{1,0:T(8,128)(2,1)}, u32[]{:S(2)}, u32[]{:S(2)}) %collective-permute-start.7) | collective-permute-done | bytes 172064 | tf_op jit(solution)/shard_map/ppermute | solution.py:513
  50.8 1.0 add_convert_fusion
  51.8 2.7 %collective-permute-start.8 = (bf16[112,384]{1,0:T(8,128)(2,1)S(1)}, bf16[112,384]{1,0:T(8,128)(2,1)S(1)}, u32[]{:S(2)}, u32[]{:S(2)}) collective-permute-start(bf16[112,384]{1,0:T(8,128)(2,1)S(1)} %broadcast_select_fusion.5), channel_id=1, source_target_pairs={{0,8},{2,10},{4,12},{6,14},{8,0},{10,2},{12,4},{14,6},{1,9},{3,11}... | collective-permute-start | bytes 258056 | tf_op jit(solution)/shard_map/ppermute | solution.py:513
  54.5 4.7 %collective-permute-done.8 = bf16[112,384]{1,0:T(8,128)(2,1)S(1)} collective-permute-done((bf16[112,384]{1,0:T(8,128)(2,1)S(1)}, bf16[112,384]{1,0:T(8,128)(2,1)S(1)}, u32[]{:S(2)}, u32[]{:S(2)}) %collective-permute-start.8) | collective-permute-done | bytes 86048 | tf_op jit(solution)/shard_map/ppermute | solution.py:513
  59.2 0.5 collective-permute-start.9
  59.8 4.0 %collective-permute-done.9 = bf16[112,384]{1,0:T(8,128)(2,1)S(1)} collective-permute-done((bf16[112,384]{1,0:T(8,128)(2,1)S(1)}, bf16[112,384]{1,0:T(8,128)(2,1)S(1)}, u32[]{:S(2)}, u32[]{:S(2)}) %collective-permute-start.9) | collective-permute-done | bytes 86048 | tf_op jit(solution)/shard_map/ppermute | solution.py:513
  63.8 0.9 collective-permute-start.10
  64.7 1.7 %shard_map.86 = bf16[384,768]{1,0:T(8,128)(2,1)S(1)} custom-call(s32[3]{0:T(128)S(1)} %add_convert_fusion.3.flags, bf16[1536,768]{1,0:T(8,128)(2,1)S(1)} %copy-done.2, bf16[1536,768]{1,0:T(8,128)(2,1)} %collective-permute-done.2.other_e), custom_call_target="tpu_custom_call" | custom-call | flops 2000000000 | bytes 6291456 | tf_op jit(solution)/shard_map/pallas_call | solution.py:419
  66.5 2.4 %collective-permute-start.3 = (bf16[384,768]{1,0:T(8,128)(2,1)S(1)}, bf16[384,768]{1,0:T(8,128)(2,1)S(1)}, u32[]{:S(2)}, u32[]{:S(2)}) collective-permute-start(bf16[384,768]{1,0:T(8,128)(2,1)S(1)} %shard_map.86), channel_id=1, source_target_pairs={{2,0},{4,2},{6,4},{8,6},{10,8},{12,10},{14,12},{3,1},{5,3},{7,5},{... | collective-permute-start | bytes 1769480 | tf_op jit(solution)/shard_map/ppermute | solution.py:509
  68.9 1.8 %shard_map.88 = bf16[768,768]{1,0:T(8,128)(2,1)S(1)} custom-call(s32[3]{0:T(128)S(1)} %add_convert_fusion.3.flags, bf16[384,1536]{1,0:T(8,128)(2,1)} %get-tuple-element.8.own_r, bf16[384,1536]{1,0:T(8,128)(2,1)} %collective-permute-done.5.other_r, bf16[1536,768]{1,0:T(8,128)(2,1)S(1)} %copy-done.2), custom_call_target="tpu_custom_call" | custom-call | flops 2000000000 | bytes 6291456 | tf_op jit(solution)/shard_map/pallas_call | solution.py:390
  70.7 2.1 %collective-permute-start.6 = (bf16[768,768]{1,0:T(8,128)(2,1)S(1)}, bf16[768,768]{1,0:T(8,128)(2,1)S(1)}, u32[]{:S(2)}, u32[]{:S(2)}) collective-permute-start(bf16[768,768]{1,0:T(8,128)(2,1)S(1)} %shard_map.88), channel_id=1, source_target_pairs={{2,0},{4,2},{6,4},{8,6},{10,8},{12,10},{14,12},{3,1},{5,3},{7,5},{... | collective-permute-start | bytes 3538952 | tf_op jit(solution)/shard_map/ppermute | solution.py:509
  72.8 5.8 %collective-permute-start.11 = (bf16[224,384]{1,0:T(8,128)(2,1)S(1)}, bf16[224,384]{1,0:T(8,128)(2,1)S(1)}, u32[]{:S(2)}, u32[]{:S(2)}) collective-permute-start(bf16[224,384]{1,0:T(8,128)(2,1)S(1)} %pad_maximum_fusion.1), channel_id=1, source_target_pairs={{0,4},{2,6},{4,0},{6,2},{8,12},{10,14},{12,8},{14,10},{1,5},{3,7},... | collective-permute-start | bytes 516104 | tf_op jit(solution)/shard_map/ppermute | solution.py:513
  78.6 1.9 %collective-permute-start.1 = (bf16[784,384]{1,0:T(8,128)(2,1)S(1)}, bf16[784,384]{1,0:T(8,128)(2,1)S(1)}, u32[]{:S(2)}, u32[]{:S(2)}) collective-permute-start(bf16[784,384]{1,0:T(8,128)(2,1)S(1)} %get-tuple-element.6), channel_id=1, source_target_pairs={{2,0},{4,2},{6,4},{8,6},{10,8},{12,10},{14,12},{3,1},{5,3},{7,5},{... | collective-permute-start | bytes 1806344 | tf_op jit(solution)/shard_map/ppermute | solution.py:509
  80.5 5.2 %collective-permute-done.3.own_cross = bf16[384,768]{1,0:T(8,128)(2,1)S(1)} collective-permute-done((bf16[384,768]{1,0:T(8,128)(2,1)S(1)}, bf16[384,768]{1,0:T(8,128)(2,1)S(1)}, u32[]{:S(2)}, u32[]{:S(2)}) %collective-permute-start.3) | collective-permute-done | bytes 589856 | tf_op jit(solution)/shard_map/ppermute | solution.py:509
  85.8 0.6 collective-permute-start.12
  86.4 1.8 %collective-permute-done.12.other_sum = bf16[448,384]{1,0:T(8,128)(2,1)S(1)} collective-permute-done((bf16[448,384]{1,0:T(8,128)(2,1)S(1)}, bf16[448,384]{1,0:T(8,128)(2,1)S(1)}, u32[]{:S(2)}, u32[]{:S(2)}) %collective-permute-start.12) | collective-permute-done | bytes 344096 | tf_op jit(solution)/shard_map/ppermute | solution.py:504
  88.2 1.8 %shard_map.90 = f32[768,384]{1,0:T(8,128)} custom-call(s32[3]{0:T(128)S(1)} %add_convert_fusion.3.flags, bf16[768,384]{1,0:T(8,128)(2,1)S(1)} %copy-done.1, bf16[448,384]{1,0:T(8,128)(2,1)S(1)} %pad_maximum_fusion.own_sum, bf16[448,384]{1,0:T(8,128)(2,1)S(1)} %collective-permute-done.12.other_sum), custom_call_target="tpu_custom_call" | custom-call | flops 1000000 | bytes 3145728 | tf_op jit(solution)/shard_map/pallas_call | solution.py:493
  90.0 21.0 %collective-permute-done.6 = bf16[768,768]{1,0:T(8,128)(2,1)S(1)} collective-permute-done((bf16[768,768]{1,0:T(8,128)(2,1)S(1)}, bf16[768,768]{1,0:T(8,128)(2,1)S(1)}, u32[]{:S(2)}, u32[]{:S(2)}) %collective-permute-start.6) | collective-permute-done | bytes 1179680 | tf_op jit(solution)/shard_map/ppermute | solution.py:509
  111.0 14.5 %collective-permute-done.1.packed = bf16[784,384]{1,0:T(8,128)(2,1)S(1)} collective-permute-done((bf16[784,384]{1,0:T(8,128)(2,1)S(1)}, bf16[784,384]{1,0:T(8,128)(2,1)S(1)}, u32[]{:S(2)}, u32[]{:S(2)}) %collective-permute-start.1) | collective-permute-done | bytes 602144 | tf_op jit(solution)/shard_map/ppermute | solution.py:509
  125.5 2.6 %shard_map.87 = bf16[1536,768]{1,0:T(8,128)(2,1)} custom-call(s32[3]{0:T(128)S(1)} %add_convert_fusion.3.flags, bf16[1536,768]{1,0:T(8,128)(2,1)S(1)} %copy-done, bf16[784,384]{1,0:T(8,128)(2,1)S(1)} %collective-permute-done.1.packed, bf16[384,768]{1,0:T(8,128)(2,1)S(1)} %collective-permute-done.3.own_cross, ...), custom_call_target="tpu_custom_call" | custom-call | flops 1000000 | bytes 6291456 | tf_op jit(solution)/shard_map/pallas_call | solution.py:461
  128.1 1.0 copy.10
  (20 shorter events, 0.3 us)
Async XLA Ops:
  0.6 4.8 %collective-permute-start = (bf16[1536,768]{1,0:T(8,128)(2,1)}, bf16[1536,768]{1,0:T(8,128)(2,1)S(1)}, u32[]{:S(2)}, u32[]{:S(2)}) collective-permute-start(bf16[1536,768]{1,0:T(8,128)(2,1)} %own_d.1), channel_id=1, source_target_pairs={{0,1},{1,0},{2,3},{3,2},{4,5},{5,4},{6,7},{7,6},{8,9},{9,8},{10,11... | collective-permute-start | bytes 7077896 | tf_op jit(solution)/shard_map/ppermute | solution.py:504
  5.4 1.4 %copy-start.3 = (bf16[1536,768]{1,0:T(8,128)(2,1)}, bf16[1536,768]{1,0:T(8,128)(2,1)S(1)}, u32[]{:S(2)}) copy-start(bf16[1536,768]{1,0:T(8,128)(2,1)S(1)} %collective-permute-done.other_d) | copy-start | bytes 7077892
  11.0 3.3 %collective-permute-start.5 = (bf16[384,1536]{1,0:T(8,128)(2,1)}, bf16[384,1536]{1,0:T(8,128)(2,1)}, u32[]{:S(2)}, u32[]{:S(2)}) collective-permute-start(bf16[384,1536]{1,0:T(8,128)(2,1)} %get-tuple-element.8.own_r), channel_id=1, source_target_pairs={{0,1},{1,0},{2,3},{3,2},{4,5},{5,4},{6,7},{7,6},{8,9},{9,8},{10,11... | collective-permute-start | bytes 3538952 | tf_op jit(solution)/shard_map/ppermute | solution.py:504
  11.2 53.5 %collective-permute-start.2 = (bf16[1536,768]{1,0:T(8,128)(2,1)}, bf16[1536,768]{1,0:T(8,128)(2,1)}, u32[]{:S(2)}, u32[]{:S(2)}) collective-permute-start(bf16[1536,768]{1,0:T(8,128)(2,1)} %get-tuple-element.7.own_e), channel_id=1, source_target_pairs={{0,1},{1,0},{2,3},{3,2},{4,5},{5,4},{6,7},{7,6},{8,9},{9,8},{10,11... | collective-permute-start | bytes 7077896 | tf_op jit(solution)/shard_map/ppermute | solution.py:504
  11.6 53.1 %copy-start.2 = (bf16[1536,768]{1,0:T(8,128)(2,1)S(1)}, bf16[1536,768]{1,0:T(8,128)(2,1)}, u32[]{:S(2)}) copy-start(bf16[1536,768]{1,0:T(8,128)(2,1)} %get-tuple-element.7.own_e) | copy-start | bytes 7077892
  16.0 34.8 %collective-permute-start.7 = (bf16[224,384]{1,0:T(8,128)(2,1)S(1)}, bf16[224,384]{1,0:T(8,128)(2,1)}, u32[]{:S(2)}, u32[]{:S(2)}) collective-permute-start(bf16[224,384]{1,0:T(8,128)(2,1)S(1)} %broadcast_select_fusion.2), channel_id=1, source_target_pairs={{0,4},{2,6},{4,0},{6,2},{8,12},{10,14},{12,8},{14,10},{1,5},{3,7},... | collective-permute-start | bytes 516104 | tf_op jit(solution)/shard_map/ppermute | solution.py:513
  51.8 7.4 %collective-permute-start.8 = (bf16[112,384]{1,0:T(8,128)(2,1)S(1)}, bf16[112,384]{1,0:T(8,128)(2,1)S(1)}, u32[]{:S(2)}, u32[]{:S(2)}) collective-permute-start(bf16[112,384]{1,0:T(8,128)(2,1)S(1)} %broadcast_select_fusion.5), channel_id=1, source_target_pairs={{0,8},{2,10},{4,12},{6,14},{8,0},{10,2},{12,4},{14,6},{1,9},{3,11}... | collective-permute-start | bytes 258056 | tf_op jit(solution)/shard_map/ppermute | solution.py:513
  59.2 4.6 %collective-permute-start.9 = (bf16[112,384]{1,0:T(8,128)(2,1)S(1)}, bf16[112,384]{1,0:T(8,128)(2,1)S(1)}, u32[]{:S(2)}, u32[]{:S(2)}) collective-permute-start(bf16[112,384]{1,0:T(8,128)(2,1)S(1)} %add_convert_fusion.2), channel_id=1, source_target_pairs={{0,2},{2,0},{4,6},{6,4},{8,10},{10,8},{12,14},{14,12},{1,3},{3,1},... | collective-permute-start | bytes 258056 | tf_op jit(solution)/shard_map/ppermute | solution.py:513
  63.8 9.0 %collective-permute-start.10 = (bf16[112,384]{1,0:T(8,128)(2,1)S(1)}, bf16[112,384]{1,0:T(8,128)(2,1)S(1)}, u32[]{:S(2)}, u32[]{:S(2)}) collective-permute-start(bf16[112,384]{1,0:T(8,128)(2,1)S(1)} %add_convert_fusion.1), channel_id=1, source_target_pairs={{0,8},{2,10},{4,12},{6,14},{8,0},{10,2},{12,4},{14,6},{1,9},{3,11}... | collective-permute-start | bytes 258056 | tf_op jit(solution)/shard_map/ppermute | solution.py:513
  66.5 19.3 %collective-permute-start.3 = (bf16[384,768]{1,0:T(8,128)(2,1)S(1)}, bf16[384,768]{1,0:T(8,128)(2,1)S(1)}, u32[]{:S(2)}, u32[]{:S(2)}) collective-permute-start(bf16[384,768]{1,0:T(8,128)(2,1)S(1)} %shard_map.86), channel_id=1, source_target_pairs={{2,0},{4,2},{6,4},{8,6},{10,8},{12,10},{14,12},{3,1},{5,3},{7,5},{... | collective-permute-start | bytes 1769480 | tf_op jit(solution)/shard_map/ppermute | solution.py:509
  68.9 19.3 %copy-start.1 = (bf16[768,384]{1,0:T(8,128)(2,1)S(1)}, bf16[768,384]{1,0:T(8,128)(2,1)}, u32[]{:S(2)}) copy-start(bf16[768,384]{1,0:T(8,128)(2,1)} %tip.1) | copy-start | bytes 1769476
  70.7 54.8 %copy-start = (bf16[1536,768]{1,0:T(8,128)(2,1)S(1)}, bf16[1536,768]{1,0:T(8,128)(2,1)}, u32[]{:S(2)}) copy-start(bf16[1536,768]{1,0:T(8,128)(2,1)} %separator.1) | copy-start | bytes 7077892
  70.7 40.3 %collective-permute-start.6 = (bf16[768,768]{1,0:T(8,128)(2,1)S(1)}, bf16[768,768]{1,0:T(8,128)(2,1)S(1)}, u32[]{:S(2)}, u32[]{:S(2)}) collective-permute-start(bf16[768,768]{1,0:T(8,128)(2,1)S(1)} %shard_map.88), channel_id=1, source_target_pairs={{2,0},{4,2},{6,4},{8,6},{10,8},{12,10},{14,12},{3,1},{5,3},{7,5},{... | collective-permute-start | bytes 3538952 | tf_op jit(solution)/shard_map/ppermute | solution.py:509
  72.8 12.9 %collective-permute-start.11 = (bf16[224,384]{1,0:T(8,128)(2,1)S(1)}, bf16[224,384]{1,0:T(8,128)(2,1)S(1)}, u32[]{:S(2)}, u32[]{:S(2)}) collective-permute-start(bf16[224,384]{1,0:T(8,128)(2,1)S(1)} %pad_maximum_fusion.1), channel_id=1, source_target_pairs={{0,4},{2,6},{4,0},{6,2},{8,12},{10,14},{12,8},{14,10},{1,5},{3,7},... | collective-permute-start | bytes 516104 | tf_op jit(solution)/shard_map/ppermute | solution.py:513
  78.6 46.9 %collective-permute-start.1 = (bf16[784,384]{1,0:T(8,128)(2,1)S(1)}, bf16[784,384]{1,0:T(8,128)(2,1)S(1)}, u32[]{:S(2)}, u32[]{:S(2)}) collective-permute-start(bf16[784,384]{1,0:T(8,128)(2,1)S(1)} %get-tuple-element.6), channel_id=1, source_target_pairs={{2,0},{4,2},{6,4},{8,6},{10,8},{12,10},{14,12},{3,1},{5,3},{7,5},{... | collective-permute-start | bytes 1806344 | tf_op jit(solution)/shard_map/ppermute | solution.py:509
  85.7 39.8 %collective-permute-start.4 = (bf16[384,768]{1,0:T(8,128)(2,1)S(1)}, bf16[384,768]{1,0:T(8,128)(2,1)S(1)}, u32[]{:S(2)}, u32[]{:S(2)}) collective-permute-start(bf16[384,768]{1,0:T(8,128)(2,1)S(1)} %collective-permute-done.3.own_cross), channel_id=1, source_target_pairs={{0,1},{1,0},{2,3},{3,2},{4,5},{5,4},{6,7},{7,6},{8,9},{9,8},{10,11... | collective-permute-start | bytes 1769480 | tf_op jit(solution)/shard_map/ppermute | solution.py:504
  85.8 2.4 %collective-permute-start.12 = (bf16[448,384]{1,0:T(8,128)(2,1)S(1)}, bf16[448,384]{1,0:T(8,128)(2,1)S(1)}, u32[]{:S(2)}, u32[]{:S(2)}) collective-permute-start(bf16[448,384]{1,0:T(8,128)(2,1)S(1)} %pad_maximum_fusion.own_sum), channel_id=1, source_target_pairs={{0,1},{1,0},{2,3},{3,2},{4,5},{5,4},{6,7},{7,6},{8,9},{9,8},{10,11... | collective-permute-start | bytes 1032200 | tf_op jit(solution)/shard_map/ppermute | solution.py:504

commit v4 on v3

--- a/solution.py
+++ b/solution.py
@@ -7,12 +7,16 @@
 from jax.experimental.pallas import tpu as pltpu
 from jax.sharding import PartitionSpec as P
 
+
 F32 = jnp.float32
 BF16 = jnp.bfloat16
 BLOCK = 256
 NEAR = 0.03
 MOST_STEPS = 60
 STAGES = 7
+PAD = 16
+PIECES = 3
+SHARDS = 4
 
 
 def split(x):
@@ -118,7 +122,7 @@
 
 
 def eliminate_kernel(
-    flags, own_d, other_d, e_hbm, r_hbm, solved_e, solved_r, packed,
+    flags, own_d, other_d, e_hbm, r_hbm, solved_e, solved_r, corner_out, folded_out,
     given, diag, e_in, r_in, left_r, high, low, factor_high, factor_low, rest_e, turned,
     near, unit_ref, root_ref, sems,
 ):
@@ -158,7 +162,8 @@
     def _():
         solved_e[...] = jnp.zeros_like(solved_e)
         solved_r[...] = jnp.zeros_like(solved_r)
-        packed[...] = jnp.zeros_like(packed)
+        corner_out[...] = jnp.zeros_like(corner_out)
+        folded_out[...] = jnp.zeros_like(folded_out)
 
     @pl.when(flags[0] != 0)
     def _():
@@ -273,9 +278,9 @@
         first = nn(turned[0:corner, :], solved_e[:, 0:corner])
         second = nn(turned[corner:width, :], solved_e[:, corner:width])
         folded, diagonal = fold(first, second, places(corner))
-        packed[0:corner, :] = folded.astype(BF16)
-        packed[corner:width, :] = nn(turned[0:corner, :], solved_e[:, corner:width]).astype(BF16)
-        packed[width:, :] = jnp.broadcast_to(diagonal, (16, corner)).astype(BF16)
+        folded_out[0:corner, :] = folded.astype(BF16)
+        folded_out[corner:, :] = jnp.broadcast_to(diagonal, (PAD, corner)).astype(BF16)
+        corner_out[...] = nn(turned[0:corner, :], solved_e[:, corner:width]).astype(BF16)
 
 
 def fold(first, second, strict):
@@ -312,10 +317,11 @@
         out_shape=(
             jax.ShapeDtypeStruct(e.shape, BF16),
             jax.ShapeDtypeStruct(r.shape, BF16),
-            jax.ShapeDtypeStruct((width + 16, width // 2), BF16),
+            jax.ShapeDtypeStruct((width // 2, width // 2), BF16),
+            jax.ShapeDtypeStruct((width // 2 + PAD, width // 2), BF16),
         ),
         in_specs=[SMEM, ANY, VMEM, ANY, ANY],
-        out_specs=(VMEM, VMEM, VMEM),
+        out_specs=(VMEM, VMEM, VMEM, VMEM),
         scratch_shapes=[
             pltpu.VMEM((size, size), BF16),
             pltpu.VMEM((size, size), F32),
@@ -333,7 +339,7 @@
             pltpu.VMEM((block, block), F32),
             pltpu.SemaphoreType.DMA((3, size // block)),
         ],
-        compiler_params=params(52),
+        compiler_params=params(46),
         cost_estimate=cost(28 * 10**9, 16 * 2**20),
     )(flags, own_d, other_d, e, r)
 
@@ -371,27 +377,40 @@
     )(flags, own_r, other_r)
 
 
-def arrow_kernel(flags, own_r, other_r, own_e, out):
+def arrow_kernel(flags, own_r, other_r, own_e, *outs):
     rows = own_r.shape[0]
-
-    @pl.when(flags[2] == 0)
-    def _():
-        out[...] = jnp.zeros_like(out)
-
-    @pl.when(flags[2] != 0)
-    def _():
-        core = flags[1]
-        for source, side in ((own_r, core), (other_r, 1 - core)):
-            place = pl.ds(pl.multiple_of(side * rows, rows), rows)
-            out[place, :] = -nn(source[...], own_e[...]).astype(BF16)
-
-
-def arrow_term(flags, own_r, other_r, own_e):
+    share = 2 * rows // len(outs)
+    active, core = flags[2], flags[1]
+
+    @pl.when(active == 0)
+    def _():
+        for out in outs:
+            out[...] = jnp.zeros_like(out)
+
+    def write(first, second):
+        for source, base in ((first, 0), (second, rows)):
+            value = (-nn(source[...], own_e[...])).astype(BF16)
+            for i, out in enumerate(outs):
+                low, high = max(base, i * share), min(base + rows, (i + 1) * share)
+                if low < high:
+                    out[low - i * share:high - i * share, :] = value[low - base:high - base, :]
+
+    @pl.when(jnp.logical_and(active != 0, core == 0))
+    def _():
+        write(own_r, other_r)
+
+    @pl.when(jnp.logical_and(active != 0, core != 0))
+    def _():
+        write(other_r, own_r)
+
+
+def arrow_terms(flags, own_r, other_r, own_e):
+    piece = jax.ShapeDtypeStruct((2 * own_r.shape[0] // PIECES, own_e.shape[1]), BF16)
     return pl.pallas_call(
         arrow_kernel,
-        out_shape=jax.ShapeDtypeStruct((2 * own_r.shape[0], own_e.shape[1]), BF16),
+        out_shape=(piece,) * PIECES,
         in_specs=[SMEM, VMEM, VMEM, VMEM],
-        out_specs=VMEM,
+        out_specs=(VMEM,) * PIECES,
         compiler_params=params(24),
         cost_estimate=cost(2 * 10**9, 6 * 2**20),
     )(flags, own_r, other_r, own_e)
@@ -426,14 +445,14 @@
     )(flags, own_e, other_e)
 
 
-def separator_kernel(flags, separator, packed, own_cross, other_cross, out):
+def separator_kernel(flags, separator, corner_in, folded, own_cross, other_cross, out):
     width = separator.shape[1]
     half = width // 2
     core = flags[1]
     first, second = unfold(
-        packed[0:half, :].astype(F32), packed[width:width + 1, :].astype(F32), places(half)
+        folded[0:half, :].astype(F32), folded[half:half + 1, :].astype(F32), places(half)
     )
-    corner = packed[half:width, :].astype(F32)
+    corner = corner_in[...].astype(F32)
     base = pl.multiple_of(core * width, width)
 
     def less(rows, columns, term):
@@ -457,15 +476,15 @@
         less(slice(0, width), right, own_cross[...].astype(F32).T)
 
 
-def separator_less(flags, separator, packed, own_cross, other_cross):
+def separator_less(flags, separator, corner, folded, own_cross, other_cross):
     return pl.pallas_call(
         separator_kernel,
         out_shape=jax.ShapeDtypeStruct(separator.shape, BF16),
-        in_specs=[SMEM, VMEM, VMEM, VMEM, VMEM],
+        in_specs=[SMEM] + [VMEM] * 5,
         out_specs=VMEM,
         compiler_params=params(24),
         cost_estimate=cost(10**6, 6 * 2**20),
-    )(flags, separator, packed, own_cross, other_cross)
+    )(flags, separator, corner, folded, own_cross, other_cross)
 
 
 def new_tip_kernel(flags, tip, own_sum, other_sum, out):
@@ -509,31 +528,46 @@
     return lax.ppermute(x, "tm", [(i, i - 1) for i in range(1, count)])
 
 
-def exchanged(x, distance):
-    return lax.ppermute(x, "tm", [(i, i ^ distance) for i in range(lax.axis_size("tm"))])
-
-
-def kept_and_sent(x, upper):
-    half = x.shape[0] // 2
-    low, high = x[:half], x[half:]
-    return jnp.where(upper, high, low), jnp.where(upper, low, high)
-
-
-def summed(x):
+def added(*terms):
+    return sum(term.astype(F32) for term in terms).astype(BF16)
+
+
+def among_odd(x, distance, cyclic):
+    count = lax.axis_size("tm") // 2
+    if cyclic:
+        group = min(SHARDS, count)
+        pairs = [(i, i // group * group + (i + distance) % group) for i in range(count)]
+    else:
+        pairs = [(i, i ^ distance) for i in range(count)]
+    return lax.ppermute(x, "tm", [(2 * i + 1, 2 * j + 1) for i, j in pairs])
+
+
+def summed(term):
     count = lax.axis_size("tm")
-    position = lax.axis_index("tm")
-    far = [1 << i for i in range(1, count.bit_length() - 1)]
-    halving = far[:2]
-    for distance in halving:
-        kept, sent = kept_and_sent(x, (position & distance) != 0)
-        x = (kept.astype(F32) + exchanged(sent, distance).astype(F32)).astype(BF16)
-    for distance in far[2:] + [1]:
-        x = (x.astype(F32) + exchanged(x, distance).astype(F32)).astype(BF16)
-    for distance in reversed(halving):
-        other = exchanged(x, distance)
-        upper = (position & distance) != 0
-        x = jnp.concatenate([jnp.where(upper, other, x), jnp.where(upper, x, other)], axis=0)
-    return x
+    term = added(term, lax.ppermute(term, "tm", [(i, i + 1) for i in range(0, count, 2)]))
+    odd_count = count // 2
+    group = min(SHARDS, odd_count)
+    place = (lax.axis_index("tm") // 2) % group
+    share = term.shape[0] // group
+    stacked = term.reshape(group, share, term.shape[1])
+
+    def shard(i):
+        return lax.dynamic_index_in_dim(stacked, i % group, 0, keepdims=False)
+
+    parts = [among_odd(shard(place + d), d, True) for d in range(1, group)]
+    own = added(shard(place), *parts)
+    distance = group
+    while distance < odd_count:
+        own = added(own, among_odd(own, distance, False))
+        distance *= 2
+    whole = jnp.zeros_like(stacked)
+    whole = lax.dynamic_update_index_in_dim(whole, own, place, 0)
+    for d in range(1, group):
+        part = among_odd(own, d, True)
+        whole = lax.dynamic_update_index_in_dim(whole, part, (place - d) % group, 0)
+    whole = whole.reshape(term.shape)
+    returned = lax.ppermute(whole, "tm", [(i + 1, i) for i in range(0, count, 2)])
+    return jnp.where(lax.axis_index("tm") % 2 == 0, returned, whole)
 
 
 def on_device(interior_diag, coupling, arrow_rows, separator_diag, tip, lengths):
@@ -543,21 +577,24 @@
         [active, lax.axis_index("space") != 0, jnp.logical_and(active, position != 0)]
     ).astype(jnp.int32)
     other_diag = swapped(interior_diag)
-    own_e, own_r, packed = eliminate(flags, interior_diag, other_diag, coupling, arrow_rows)
-    packed = to_previous(packed)
+    own_e, own_r, corner, folded = eliminate(flags, interior_diag, other_diag, coupling, arrow_rows)
+    corner = to_previous(corner)
+    other_r = swapped(own_r)
+    term = tip_term(flags, own_r, other_r)
+    tip_sum = summed(term)
+    folded = to_previous(folded)
     other_e = swapped(own_e)
-    other_r = swapped(own_r)
     cross = cross_term(flags, own_e, other_e)
     cross = to_previous(cross)
-    arrow = arrow_term(flags, own_r, other_r, own_e)
-    arrow_fill = to_previous(arrow)
-    term = tip_term(flags, own_r, other_r)
-    tip_sum = summed(term)
+    pieces = arrow_terms(flags, own_r, other_r, own_e)
+    received = []
+    for piece in pieces:
+        received.append(to_previous(piece))
     other_cross = swapped(cross)
-    new_separator = separator_less(flags, separator_diag, packed, cross, other_cross)
+    new_separator = separator_less(flags, separator_diag, corner, folded, cross, other_cross)
     other_sum = swapped(tip_sum)
     new_tip = tip_less(flags, tip, tip_sum, other_sum)
-    return (new_separator, arrow_fill, new_tip)
+    return (new_separator, jnp.concatenate(received, axis=0), new_tip)
 
 
 def solution(mesh):

time: 129 us -> 153 us (1.19)
  the two profiles are of different devices: /device:TPU:2 before, /device:TPU:0 now
where the time goes in v4:
time: 153 us
  waiting for transfers between devices  80 us (52%)
  Pallas kernels  39 us (25%)
  starting transfers between devices  17.1 us (11%)
  local copies, waits for them, and re-layouts  8.78 us (6%)
  other arithmetic  6.09 us (4%)
  between operations  1.62 us (1%)
    ppermute x6, waiting for transfers between devices, to_previous(): return lax.ppermute(x, 'tm', [(i, i - 1) for i in range(1, count)])  60.2 us
    pallas_call x1, Pallas kernels, eliminate(): pl.pallas_call(eliminate_kernel, out_shape=(jax.ShapeDtypeStruct(e.shape,...  29.1 us
    ppermute x6, starting transfers between devices, to_previous(): return lax.ppermute(x, 'tm', [(i, i - 1) for i in range(1, count)])  7.97 us
    ppermute x1, waiting for transfers between devices, summed(): lax.ppermute(whole, 'tm', [(i + 1, i) for i in range(0, count, 2)])  7.48 us
    ppermute x1, waiting for transfers between devices, summed(): lax.ppermute(term, 'tm', [(i, i + 1) for i in range(0, count, 2)])  7.39 us
    unnamed x22, local copies, waits for them, and re-layouts  6.16 us
    ppermute x5, waiting for transfers between devices, swapped(): return lax.ppermute(x, 'space', [(0, 1), (1, 0)])  4.88 us
    ppermute x6, starting transfers between devices, among_odd(): return lax.ppermute(x, 'tm', [(2 * i + 1, 2 * j + 1) for i, j in pairs])  4.61 us
  transfers between devices with their start and end apart: 19, of which 9 were waited for; matrix products, arithmetic and copies ran while one was open for 6% of the time, Pallas kernels for 5%

profile of v4, /device:TPU:0, one launch (start us, length us, event | category | flops | bytes accessed | tf_op | source)
XLA Modules:
  0.0 152.5 jit_solution(6216342640477906974)
XLA Ops:
  1.2 1.2 dynamic_slice.16
  3.2 2.5 %collective-permute-done.other_d = bf16[1536,768]{1,0:T(8,128)(2,1)} collective-permute-done((bf16[1536,768]{1,0:T(8,128)(2,1)}, bf16[1536,768]{1,0:T(8,128)(2,1)}, u32[]{:S(2)}, u32[]{:S(2)}) %collective-permute-start) | collective-permute-done | bytes 2359328 | tf_op jit(solution)/shard_map/ppermute | solution.py:523
  5.7 1.7 %copy-done.2 = bf16[1536,768]{1,0:T(8,128)(2,1)S(1)} copy-done((bf16[1536,768]{1,0:T(8,128)(2,1)S(1)}, bf16[1536,768]{1,0:T(8,128)(2,1)}, u32[]{:S(2)}) %copy-start.2) | copy-done | bytes 2359320
  7.4 1.3 copy-done.3
  8.6 29.1 %shard_map.85 = (bf16[1536,768]{1,0:T(8,128)(2,1)S(1)}, bf16[384,1536]{1,0:T(8,128)(2,1)S(1)}, bf16[384,384]{1,0:T(8,128)(2,1)S(1)}, bf16[400,384]{1,0:T(8,128)(2,1)S(1)}) custom-call(s32[3]{0:T(128)S(1)} %add_convert_fusion.1.flags, bf16[1536,768]{1,0:T(8,128)(2,1)S(1)} %copy-done.2, bf16[1536,768]{1,0:T(8,128)(2,1)} %collective-permute-done.other_d, ...), custom_call_target="tpu_custom_call" | custom-call | flops 28000000000 | bytes 16777216 | tf_op jit(solution)/shard_map/pallas_call | solution.py:315
  38.3 2.3 %collective-permute-done.6.other_r = bf16[384,1536]{1,0:T(8,128)(2,1)S(1)} collective-permute-done((bf16[384,1536]{1,0:T(8,128)(2,1)S(1)}, bf16[384,1536]{1,0:T(8,128)(2,1)S(1)}, u32[]{:S(2)}, u32[]{:S(2)}) %collective-permute-start.6) | collective-permute-done | bytes 1179680 | tf_op jit(solution)/shard_map/ppermute | solution.py:523
  40.6 1.3 shard_map.89
  42.0 1.0 copy-done.4
  43.0 2.0 %collective-permute-start.10 = (bf16[448,384]{1,0:T(8,128)(2,1)S(1)}, bf16[448,384]{1,0:T(8,128)(2,1)}, u32[]{:S(2)}, u32[]{:S(2)}) collective-permute-start(bf16[448,384]{1,0:T(8,128)(2,1)S(1)} %shard_map.89), channel_id=1, source_target_pairs={{0,2},{4,6},{8,10},{12,14},{1,3},{5,7},{9,11},{13,15},{16,18},{20,... | collective-permute-start | bytes 1032200 | tf_op jit(solution)/shard_map/ppermute | solution.py:547
  45.1 7.4 %collective-permute-done.10 = bf16[448,384]{1,0:T(8,128)(2,1)} collective-permute-done((bf16[448,384]{1,0:T(8,128)(2,1)S(1)}, bf16[448,384]{1,0:T(8,128)(2,1)}, u32[]{:S(2)}, u32[]{:S(2)}) %collective-permute-start.10) | collective-permute-done | bytes 344096 | tf_op jit(solution)/shard_map/ppermute | solution.py:547
  52.4 1.1 add_convert_fusion
  55.6 1.3 collective-permute-start.11
  57.0 1.6 %bitcast_dynamic-update-slice_fusion.3 = (bf16[4,112,384]{2,1,0:T(8,128)(2,1)S(1)}, bf16[112,384]{1,0:T(8,128)(2,1)}) fusion(bf16[4,112,384]{2,1,0:T(8,128)(2,1)S(1)} %broadcast_in_dim.16, s32[]{:T(128)S(6)} %select_n.93, bf16[112,384]{1,0:T(8,128)(2,1)S(1)} %collective-permute-done.13, bf16[112,384]{1,0:T(8,128)(2,1)S(1)} %collective-permute-done.12, ...), kind=kLoop, calls=%fused_computation.10 | loop fusion | flops 344064 | bytes 516104 | tf_op jit(solution)/shard_map/jit(dynamic_update_index_in_dim)/dynamic_update_slice | solution.py:564
  61.4 2.6 %shard_map.86 = bf16[384,768]{1,0:T(8,128)(2,1)} custom-call(s32[3]{0:T(128)S(1)} %add_convert_fusion.1.flags, bf16[1536,768]{1,0:T(8,128)(2,1)S(1)} %get-tuple-element.12.own_e, bf16[1536,768]{1,0:T(8,128)(2,1)} %collective-permute-done.3.other_e), custom_call_target="tpu_custom_call" | custom-call | flops 2000000000 | bytes 6291456 | tf_op jit(solution)/shard_map/pallas_call | solution.py:438
  64.1 1.3 collective-permute-start.4
  66.7 1.3 collective-permute-start.17
  68.0 1.5 shard_map.88
  70.3 1.4 collective-permute-start.9
  71.7 1.3 collective-permute-start.8
  73.0 1.3 collective-permute-start.7
  74.3 33.0 %collective-permute-done.4.own_cross = bf16[384,768]{1,0:T(8,128)(2,1)S(1)} collective-permute-done((bf16[384,768]{1,0:T(8,128)(2,1)}, bf16[384,768]{1,0:T(8,128)(2,1)S(1)}, u32[]{:S(2)}, u32[]{:S(2)}) %collective-permute-start.4) | collective-permute-done | bytes 589856 | tf_op jit(solution)/shard_map/ppermute | solution.py:528
  107.3 7.5 %collective-permute-done.17 = bf16[448,384]{1,0:T(8,128)(2,1)} collective-permute-done((bf16[448,384]{1,0:T(8,128)(2,1)}, bf16[448,384]{1,0:T(8,128)(2,1)}, u32[]{:S(2)}, u32[]{:S(2)}) %collective-permute-start.17) | collective-permute-done | bytes 344096 | tf_op jit(solution)/shard_map/ppermute | solution.py:569
  114.8 1.1 broadcast_select_fusion.own_sum
  116.0 7.2 %collective-permute-done.9 = bf16[256,768]{1,0:T(8,128)(2,1)} collective-permute-done((bf16[256,768]{1,0:T(8,128)(2,1)}, bf16[256,768]{1,0:T(8,128)(2,1)}, u32[]{:S(2)}, u32[]{:S(2)}) %collective-permute-start.9) | collective-permute-done | bytes 393248 | tf_op jit(solution)/shard_map/ppermute | solution.py:528
  123.2 1.3 collective-permute-start.2
  124.5 7.1 %collective-permute-done.8 = bf16[256,768]{1,0:T(8,128)(2,1)} collective-permute-done((bf16[256,768]{1,0:T(8,128)(2,1)}, bf16[256,768]{1,0:T(8,128)(2,1)}, u32[]{:S(2)}, u32[]{:S(2)}) %collective-permute-start.8) | collective-permute-done | bytes 393248 | tf_op jit(solution)/shard_map/ppermute | solution.py:528
  131.7 1.4 collective-permute-start.1
  133.1 6.9 %collective-permute-done.7 = bf16[256,768]{1,0:T(8,128)(2,1)S(1)} collective-permute-done((bf16[256,768]{1,0:T(8,128)(2,1)}, bf16[256,768]{1,0:T(8,128)(2,1)S(1)}, u32[]{:S(2)}, u32[]{:S(2)}) %collective-permute-start.7) | collective-permute-done | bytes 393248 | tf_op jit(solution)/shard_map/ppermute | solution.py:528
  140.0 2.2 %pad_maximum_fusion = bf16[768,768]{1,0:T(8,128)(2,1)} fusion(bf16[256,768]{1,0:T(8,128)(2,1)} %collective-permute-done.9, bf16[256,768]{1,0:T(8,128)(2,1)} %collective-permute-done.8, bf16[256,768]{1,0:T(8,128)(2,1)S(1)} %collective-permute-done.7), kind=kLoop, calls=%fused_computation | loop fusion | flops 3538944 | bytes 2359296 | tf_op jit(solution)/shard_map/concatenate | solution.py:597
  142.2 1.8 %shard_map.90 = f32[768,384]{1,0:T(8,128)} custom-call(s32[3]{0:T(128)S(1)} %add_convert_fusion.1.flags, bf16[768,384]{1,0:T(8,128)(2,1)S(1)} %copy-done.1, bf16[448,384]{1,0:T(8,128)(2,1)S(1)} %broadcast_select_fusion.own_sum, bf16[448,384]{1,0:T(8,128)(2,1)S(1)} %collective-permute-done.18.other_sum), custom_call_target="tpu_custom_call" | custom-call | flops 1000000 | bytes 3145728 | tf_op jit(solution)/shard_map/pallas_call | solution.py:512
  144.0 5.9 %collective-permute-done.1.corner_in = bf16[384,384]{1,0:T(8,128)(2,1)S(1)} collective-permute-done((bf16[384,384]{1,0:T(8,128)(2,1)S(1)}, bf16[384,384]{1,0:T(8,128)(2,1)S(1)}, u32[]{:S(2)}, u32[]{:S(2)}) %collective-permute-start.1) | collective-permute-done | bytes 294944 | tf_op jit(solution)/shard_map/ppermute | solution.py:528
  149.9 2.6 %shard_map.87 = bf16[1536,768]{1,0:T(8,128)(2,1)} custom-call(s32[3]{0:T(128)S(1)} %add_convert_fusion.1.flags, bf16[1536,768]{1,0:T(8,128)(2,1)S(1)} %copy-done, bf16[384,384]{1,0:T(8,128)(2,1)S(1)} %collective-permute-done.1.corner_in, bf16[400,384]{1,0:T(8,128)(2,1)S(1)} %collective-permute-done.2.folded, ...), custom_call_target="tpu_custom_call" | custom-call | flops 1000000 | bytes 6291456 | tf_op jit(solution)/shard_map/pallas_call | solution.py:480
  (45 shorter events, 8.2 us)
Async XLA Ops:
  0.6 5.1 %collective-permute-start = (bf16[1536,768]{1,0:T(8,128)(2,1)}, bf16[1536,768]{1,0:T(8,128)(2,1)}, u32[]{:S(2)}, u32[]{:S(2)}) collective-permute-start(bf16[1536,768]{1,0:T(8,128)(2,1)} %own_d.1), channel_id=1, source_target_pairs={{0,1},{1,0},{2,3},{3,2},{4,5},{5,4},{6,7},{7,6},{8,9},{9,8},{10,11... | collective-permute-start | bytes 7077896 | tf_op jit(solution)/shard_map/ppermute | solution.py:523
  5.7 1.7 %copy-start.2 = (bf16[1536,768]{1,0:T(8,128)(2,1)S(1)}, bf16[1536,768]{1,0:T(8,128)(2,1)}, u32[]{:S(2)}) copy-start(bf16[1536,768]{1,0:T(8,128)(2,1)} %own_d.1) | copy-start | bytes 7077892
  7.4 1.3 copy-start.3
  37.7 2.9 %collective-permute-start.6 = (bf16[384,1536]{1,0:T(8,128)(2,1)S(1)}, bf16[384,1536]{1,0:T(8,128)(2,1)S(1)}, u32[]{:S(2)}, u32[]{:S(2)}) collective-permute-start(bf16[384,1536]{1,0:T(8,128)(2,1)S(1)} %get-tuple-element.13.own_r), channel_id=1, source_target_pairs={{0,1},{1,0},{2,3},{3,2},{4,5},{5,4},{6,7},{7,6},{8,9},{9,8},{10,11... | collective-permute-start | bytes 3538952 | tf_op jit(solution)/shard_map/ppermute | solution.py:523
  38.2 22.6 %collective-permute-start.3 = (bf16[1536,768]{1,0:T(8,128)(2,1)S(1)}, bf16[1536,768]{1,0:T(8,128)(2,1)}, u32[]{:S(2)}, u32[]{:S(2)}) collective-permute-start(bf16[1536,768]{1,0:T(8,128)(2,1)S(1)} %get-tuple-element.12.own_e), channel_id=1, source_target_pairs={{0,1},{1,0},{2,3},{3,2},{4,5},{5,4},{6,7},{7,6},{8,9},{9,8},{10,11... | collective-permute-start | bytes 7077896 | tf_op jit(solution)/shard_map/ppermute | solution.py:523
  40.6 1.4 copy-start.6
  42.0 1.0 copy-start.4
  43.0 9.4 %collective-permute-start.10 = (bf16[448,384]{1,0:T(8,128)(2,1)S(1)}, bf16[448,384]{1,0:T(8,128)(2,1)}, u32[]{:S(2)}, u32[]{:S(2)}) collective-permute-start(bf16[448,384]{1,0:T(8,128)(2,1)S(1)} %shard_map.89), channel_id=1, source_target_pairs={{0,2},{4,6},{8,10},{12,14},{1,3},{5,7},{9,11},{13,15},{16,18},{20,... | collective-permute-start | bytes 1032200 | tf_op jit(solution)/shard_map/ppermute | solution.py:547
  53.5 0.7 copy-start.9
  54.3 2.6 %collective-permute-start.13 = (bf16[112,384]{1,0:T(8,128)(2,1)S(1)}, bf16[112,384]{1,0:T(8,128)(2,1)S(1)}, u32[]{:S(2)}, u32[]{:S(2)}) collective-permute-start(bf16[112,384]{1,0:T(8,128)(2,1)S(1)} %get-tuple-element.20), channel_id=1, source_target_pairs={{2,14},{6,2},{10,6},{14,10},{3,15},{7,3},{11,7},{15,11},{18,30},{2... | collective-permute-start | bytes 258056 | tf_op jit(solution)/shard_map/ppermute | solution.py:542
  54.9 2.0 %collective-permute-start.12 = (bf16[112,384]{1,0:T(8,128)(2,1)S(1)}, bf16[112,384]{1,0:T(8,128)(2,1)S(1)}, u32[]{:S(2)}, u32[]{:S(2)}) collective-permute-start(bf16[112,384]{1,0:T(8,128)(2,1)S(1)} %get-tuple-element.21), channel_id=1, source_target_pairs={{2,10},{6,14},{10,2},{14,6},{3,11},{7,15},{11,3},{15,7},{18,26},{2... | collective-permute-start | bytes 258056 | tf_op jit(solution)/shard_map/ppermute | solution.py:542
  55.6 1.3 collective-permute-start.11
  58.6 2.1 %collective-permute-start.14 = (bf16[112,384]{1,0:T(8,128)(2,1)}, bf16[112,384]{1,0:T(8,128)(2,1)S(1)}, u32[]{:S(2)}, u32[]{:S(2)}) collective-permute-start(bf16[112,384]{1,0:T(8,128)(2,1)} %get-tuple-element.18), channel_id=1, source_target_pairs={{2,6},{6,10},{10,14},{14,2},{3,7},{7,11},{11,15},{15,3},{18,22},{2... | collective-permute-start | bytes 258056 | tf_op jit(solution)/shard_map/ppermute | solution.py:542
  59.3 6.1 %collective-permute-start.15 = (bf16[112,384]{1,0:T(8,128)(2,1)}, bf16[112,384]{1,0:T(8,128)(2,1)S(1)}, u32[]{:S(2)}, u32[]{:S(2)}) collective-permute-start(bf16[112,384]{1,0:T(8,128)(2,1)} %get-tuple-element.18), channel_id=1, source_target_pairs={{2,10},{6,14},{10,2},{14,6},{3,11},{7,15},{11,3},{15,7},{18,26},{2... | collective-permute-start | bytes 258056 | tf_op jit(solution)/shard_map/ppermute | solution.py:542
  60.0 6.1 %collective-permute-start.16 = (bf16[112,384]{1,0:T(8,128)(2,1)}, bf16[112,384]{1,0:T(8,128)(2,1)S(1)}, u32[]{:S(2)}, u32[]{:S(2)}) collective-permute-start(bf16[112,384]{1,0:T(8,128)(2,1)} %get-tuple-element.18), channel_id=1, source_target_pairs={{2,14},{6,2},{10,6},{14,10},{3,15},{7,3},{11,7},{15,11},{18,30},{2... | collective-permute-start | bytes 258056 | tf_op jit(solution)/shard_map/ppermute | solution.py:542
  60.7 0.7 copy-start.10
  60.7 7.3 %copy-start.5 = (bf16[384,1536]{1,0:T(8,128)(2,1)S(1)}, bf16[384,1536]{1,0:T(8,128)(2,1)}, u32[]{:S(2)}) copy-start(bf16[384,1536]{1,0:T(8,128)(2,1)} %copy-done.4) | copy-start | bytes 3538948
  60.7 7.3 %copy-start.7 = (bf16[384,1536]{1,0:T(8,128)(2,1)S(1)}, bf16[384,1536]{1,0:T(8,128)(2,1)}, u32[]{:S(2)}) copy-start(bf16[384,1536]{1,0:T(8,128)(2,1)} %copy-done.6) | copy-start | bytes 3538948
  64.1 43.2 %collective-permute-start.4 = (bf16[384,768]{1,0:T(8,128)(2,1)}, bf16[384,768]{1,0:T(8,128)(2,1)S(1)}, u32[]{:S(2)}, u32[]{:S(2)}) collective-permute-start(bf16[384,768]{1,0:T(8,128)(2,1)} %shard_map.86), channel_id=1, source_target_pairs={{2,0},{4,2},{6,4},{8,6},{10,8},{12,10},{14,12},{3,1},{5,3},{7,5},{... | collective-permute-start | bytes 1769480 | tf_op jit(solution)/shard_map/ppermute | solution.py:528
  66.7 48.1 %collective-permute-start.17 = (bf16[448,384]{1,0:T(8,128)(2,1)}, bf16[448,384]{1,0:T(8,128)(2,1)}, u32[]{:S(2)}, u32[]{:S(2)}) collective-permute-start(bf16[448,384]{1,0:T(8,128)(2,1)} %bitcast.26), channel_id=1, source_target_pairs={{2,0},{6,4},{10,8},{14,12},{3,1},{7,5},{11,9},{15,13},{18,16},{22,... | collective-permute-start | bytes 1032200 | tf_op jit(solution)/shard_map/ppermute | solution.py:569
  69.5 0.8 copy-start.8
  70.3 71.9 %copy-start.1 = (bf16[768,384]{1,0:T(8,128)(2,1)S(1)}, bf16[768,384]{1,0:T(8,128)(2,1)}, u32[]{:S(2)}) copy-start(bf16[768,384]{1,0:T(8,128)(2,1)} %tip.1) | copy-start | bytes 1769476
  70.3 53.0 %collective-permute-start.9 = (bf16[256,768]{1,0:T(8,128)(2,1)}, bf16[256,768]{1,0:T(8,128)(2,1)}, u32[]{:S(2)}, u32[]{:S(2)}) collective-permute-start(bf16[256,768]{1,0:T(8,128)(2,1)} %get-tuple-element.16), channel_id=1, source_target_pairs={{2,0},{4,2},{6,4},{8,6},{10,8},{12,10},{14,12},{3,1},{5,3},{7,5},{... | collective-permute-start | bytes 1179656 | tf_op jit(solution)/shard_map/ppermute | solution.py:528
  71.7 60.0 %collective-permute-start.8 = (bf16[256,768]{1,0:T(8,128)(2,1)}, bf16[256,768]{1,0:T(8,128)(2,1)}, u32[]{:S(2)}, u32[]{:S(2)}) collective-permute-start(bf16[256,768]{1,0:T(8,128)(2,1)} %get-tuple-element.15), channel_id=1, source_target_pairs={{2,0},{4,2},{6,4},{8,6},{10,8},{12,10},{14,12},{3,1},{5,3},{7,5},{... | collective-permute-start | bytes 1179656 | tf_op jit(solution)/shard_map/ppermute | solution.py:528
  73.0 67.0 %collective-permute-start.7 = (bf16[256,768]{1,0:T(8,128)(2,1)}, bf16[256,768]{1,0:T(8,128)(2,1)S(1)}, u32[]{:S(2)}, u32[]{:S(2)}) collective-permute-start(bf16[256,768]{1,0:T(8,128)(2,1)} %copy-done.8), channel_id=1, source_target_pairs={{2,0},{4,2},{6,4},{8,6},{10,8},{12,10},{14,12},{3,1},{5,3},{7,5},{... | collective-permute-start | bytes 1179656 | tf_op jit(solution)/shard_map/ppermute | solution.py:528
  107.3 42.6 %collective-permute-start.5 = (bf16[384,768]{1,0:T(8,128)(2,1)S(1)}, bf16[384,768]{1,0:T(8,128)(2,1)S(1)}, u32[]{:S(2)}, u32[]{:S(2)}) collective-permute-start(bf16[384,768]{1,0:T(8,128)(2,1)S(1)} %collective-permute-done.4.own_cross), channel_id=1, source_target_pairs={{0,1},{1,0},{2,3},{3,2},{4,5},{5,4},{6,7},{7,6},{8,9},{9,8},{10,11... | collective-permute-start | bytes 1769480 | tf_op jit(solution)/shard_map/ppermute | solution.py:523
  115.9 26.3 %collective-permute-start.18 = (bf16[448,384]{1,0:T(8,128)(2,1)S(1)}, bf16[448,384]{1,0:T(8,128)(2,1)S(1)}, u32[]{:S(2)}, u32[]{:S(2)}) collective-permute-start(bf16[448,384]{1,0:T(8,128)(2,1)S(1)} %broadcast_select_fusion.own_sum), channel_id=1, source_target_pairs={{0,1},{1,0},{2,3},{3,2},{4,5},{5,4},{6,7},{7,6},{8,9},{9,8},{10,11... | collective-permute-start | bytes 1032200 | tf_op jit(solution)/shard_map/ppermute | solution.py:523
  123.2 26.7 %collective-permute-start.2 = (bf16[400,384]{1,0:T(8,128)(2,1)S(1)}, bf16[400,384]{1,0:T(8,128)(2,1)S(1)}, u32[]{:S(2)}, u32[]{:S(2)}) collective-permute-start(bf16[400,384]{1,0:T(8,128)(2,1)S(1)} %get-tuple-element.11), channel_id=1, source_target_pairs={{2,0},{4,2},{6,4},{8,6},{10,8},{12,10},{14,12},{3,1},{5,3},{7,5},{... | collective-permute-start | bytes 921608 | tf_op jit(solution)/shard_map/ppermute | solution.py:528
  131.7 18.2 %copy-start = (bf16[1536,768]{1,0:T(8,128)(2,1)S(1)}, bf16[1536,768]{1,0:T(8,128)(2,1)}, u32[]{:S(2)}) copy-start(bf16[1536,768]{1,0:T(8,128)(2,1)} %separator.1) | copy-start | bytes 7077892
  131.7 18.2 %collective-permute-start.1 = (bf16[384,384]{1,0:T(8,128)(2,1)S(1)}, bf16[384,384]{1,0:T(8,128)(2,1)S(1)}, u32[]{:S(2)}, u32[]{:S(2)}) collective-permute-start(bf16[384,384]{1,0:T(8,128)(2,1)S(1)} %get-tuple-element.10), channel_id=1, source_target_pairs={{2,0},{4,2},{6,4},{8,6},{10,8},{12,10},{14,12},{3,1},{5,3},{7,5},{... | collective-permute-start | bytes 884744 | tf_op jit(solution)/shard_map/ppermute | solution.py:528

commit v5 on v3

--- a/solution.py
+++ b/solution.py
@@ -7,12 +7,14 @@
 from jax.experimental.pallas import tpu as pltpu
 from jax.sharding import PartitionSpec as P
 
+
 F32 = jnp.float32
 BF16 = jnp.bfloat16
 BLOCK = 256
 NEAR = 0.03
 MOST_STEPS = 60
 STAGES = 7
+PAD = 16
 
 
 def split(x):
@@ -118,7 +120,7 @@
 
 
 def eliminate_kernel(
-    flags, own_d, other_d, e_hbm, r_hbm, solved_e, solved_r, packed,
+    flags, own_d, other_d, e_hbm, r_hbm, solved_e, solved_r, corner_out, folded_out,
     given, diag, e_in, r_in, left_r, high, low, factor_high, factor_low, rest_e, turned,
     near, unit_ref, root_ref, sems,
 ):
@@ -158,7 +160,8 @@
     def _():
         solved_e[...] = jnp.zeros_like(solved_e)
         solved_r[...] = jnp.zeros_like(solved_r)
-        packed[...] = jnp.zeros_like(packed)
+        corner_out[...] = jnp.zeros_like(corner_out)
+        folded_out[...] = jnp.zeros_like(folded_out)
 
     @pl.when(flags[0] != 0)
     def _():
@@ -273,9 +276,9 @@
         first = nn(turned[0:corner, :], solved_e[:, 0:corner])
         second = nn(turned[corner:width, :], solved_e[:, corner:width])
         folded, diagonal = fold(first, second, places(corner))
-        packed[0:corner, :] = folded.astype(BF16)
-        packed[corner:width, :] = nn(turned[0:corner, :], solved_e[:, corner:width]).astype(BF16)
-        packed[width:, :] = jnp.broadcast_to(diagonal, (16, corner)).astype(BF16)
+        folded_out[0:corner, :] = folded.astype(BF16)
+        folded_out[corner:, :] = jnp.broadcast_to(diagonal, (PAD, corner)).astype(BF16)
+        corner_out[...] = nn(turned[0:corner, :], solved_e[:, corner:width]).astype(BF16)
 
 
 def fold(first, second, strict):
@@ -312,10 +315,11 @@
         out_shape=(
             jax.ShapeDtypeStruct(e.shape, BF16),
             jax.ShapeDtypeStruct(r.shape, BF16),
-            jax.ShapeDtypeStruct((width + 16, width // 2), BF16),
+            jax.ShapeDtypeStruct((width // 2, width // 2), BF16),
+            jax.ShapeDtypeStruct((width // 2 + PAD, width // 2), BF16),
         ),
         in_specs=[SMEM, ANY, VMEM, ANY, ANY],
-        out_specs=(VMEM, VMEM, VMEM),
+        out_specs=(VMEM, VMEM, VMEM, VMEM),
         scratch_shapes=[
             pltpu.VMEM((size, size), BF16),
             pltpu.VMEM((size, size), F32),
@@ -333,7 +337,7 @@
             pltpu.VMEM((block, block), F32),
             pltpu.SemaphoreType.DMA((3, size // block)),
         ],
-        compiler_params=params(52),
+        compiler_params=params(54),
         cost_estimate=cost(28 * 10**9, 16 * 2**20),
     )(flags, own_d, other_d, e, r)
 
@@ -383,7 +387,7 @@
         core = flags[1]
         for source, side in ((own_r, core), (other_r, 1 - core)):
             place = pl.ds(pl.multiple_of(side * rows, rows), rows)
-            out[place, :] = -nn(source[...], own_e[...]).astype(BF16)
+            out[place, :] = (-nn(source[...], own_e[...])).astype(BF16)
 
 
 def arrow_term(flags, own_r, other_r, own_e):
@@ -426,14 +430,14 @@
     )(flags, own_e, other_e)
 
 
-def separator_kernel(flags, separator, packed, own_cross, other_cross, out):
+def separator_kernel(flags, separator, corner_in, folded, own_cross, other_cross, out):
     width = separator.shape[1]
     half = width // 2
     core = flags[1]
     first, second = unfold(
-        packed[0:half, :].astype(F32), packed[width:width + 1, :].astype(F32), places(half)
+        folded[0:half, :].astype(F32), folded[half:half + 1, :].astype(F32), places(half)
     )
-    corner = packed[half:width, :].astype(F32)
+    corner = corner_in[...].astype(F32)
     base = pl.multiple_of(core * width, width)
 
     def less(rows, columns, term):
@@ -457,15 +461,15 @@
         less(slice(0, width), right, own_cross[...].astype(F32).T)
 
 
-def separator_less(flags, separator, packed, own_cross, other_cross):
+def separator_less(flags, separator, corner, folded, own_cross, other_cross):
     return pl.pallas_call(
         separator_kernel,
         out_shape=jax.ShapeDtypeStruct(separator.shape, BF16),
-        in_specs=[SMEM, VMEM, VMEM, VMEM, VMEM],
+        in_specs=[SMEM] + [VMEM] * 5,
         out_specs=VMEM,
         compiler_params=params(24),
         cost_estimate=cost(10**6, 6 * 2**20),
-    )(flags, separator, packed, own_cross, other_cross)
+    )(flags, separator, corner, folded, own_cross, other_cross)
 
 
 def new_tip_kernel(flags, tip, own_sum, other_sum, out):
@@ -509,33 +513,6 @@
     return lax.ppermute(x, "tm", [(i, i - 1) for i in range(1, count)])
 
 
-def exchanged(x, distance):
-    return lax.ppermute(x, "tm", [(i, i ^ distance) for i in range(lax.axis_size("tm"))])
-
-
-def kept_and_sent(x, upper):
-    half = x.shape[0] // 2
-    low, high = x[:half], x[half:]
-    return jnp.where(upper, high, low), jnp.where(upper, low, high)
-
-
-def summed(x):
-    count = lax.axis_size("tm")
-    position = lax.axis_index("tm")
-    far = [1 << i for i in range(1, count.bit_length() - 1)]
-    halving = far[:2]
-    for distance in halving:
-        kept, sent = kept_and_sent(x, (position & distance) != 0)
-        x = (kept.astype(F32) + exchanged(sent, distance).astype(F32)).astype(BF16)
-    for distance in far[2:] + [1]:
-        x = (x.astype(F32) + exchanged(x, distance).astype(F32)).astype(BF16)
-    for distance in reversed(halving):
-        other = exchanged(x, distance)
-        upper = (position & distance) != 0
-        x = jnp.concatenate([jnp.where(upper, other, x), jnp.where(upper, x, other)], axis=0)
-    return x
-
-
 def on_device(interior_diag, coupling, arrow_rows, separator_diag, tip, lengths):
     position = lax.axis_index("tm")
     active = lengths[position] == 2
@@ -543,8 +520,9 @@
         [active, lax.axis_index("space") != 0, jnp.logical_and(active, position != 0)]
     ).astype(jnp.int32)
     other_diag = swapped(interior_diag)
-    own_e, own_r, packed = eliminate(flags, interior_diag, other_diag, coupling, arrow_rows)
-    packed = to_previous(packed)
+    own_e, own_r, corner, folded = eliminate(flags, interior_diag, other_diag, coupling, arrow_rows)
+    corner = to_previous(corner)
+    folded = to_previous(folded)
     other_e = swapped(own_e)
     other_r = swapped(own_r)
     cross = cross_term(flags, own_e, other_e)
@@ -552,9 +530,9 @@
     arrow = arrow_term(flags, own_r, other_r, own_e)
     arrow_fill = to_previous(arrow)
     term = tip_term(flags, own_r, other_r)
-    tip_sum = summed(term)
+    tip_sum = lax.psum(term, "tm")
     other_cross = swapped(cross)
-    new_separator = separator_less(flags, separator_diag, packed, cross, other_cross)
+    new_separator = separator_less(flags, separator_diag, corner, folded, cross, other_cross)
     other_sum = swapped(tip_sum)
     new_tip = tip_less(flags, tip, tip_sum, other_sum)
     return (new_separator, arrow_fill, new_tip)

time: 129 us -> 174 us (1.35); the launches traced: 129 us -> 172 us
  waiting for transfers between devices: 61.9 us -> 98.3 us
  between operations: 1.45 us -> 14.8 us
  starting transfers between devices: 47 us -> 36.1 us
  local copies, waits for them, and re-layouts: 3.68 us -> 9.99 us
    psum x0 -> x1, waiting for transfers between devices: none -> 43.7 us  [on_device(): tip_sum = lax.psum(term, 'tm')]
    ppermute x5 -> x0, starting transfers between devices: 39.4 us -> none  [exchanged(): lax.ppermute(x, 'tm', [(i, i ^ distance) for i in range(lax.axis_size('tm...]
    ppermute x3 -> x4, starting transfers between devices: 6.4 us -> 35.5 us  [to_previous(): return lax.ppermute(x, 'tm', [(i, i - 1) for i in range(1, count)])]
    ppermute x5 -> x0, waiting for transfers between devices: 14 us -> none  [exchanged(): lax.ppermute(x, 'tm', [(i, i ^ distance) for i in range(lax.axis_size('tm...]
    unnamed x9 -> x15, local copies, waits for them, and re-layouts: 2.43 us -> 8.75 us
    ppermute x3 -> x4, waiting for transfers between devices: 40.6 us -> 46.4 us  [to_previous(): return lax.ppermute(x, 'tm', [(i, i - 1) for i in range(1, count)])]
  transfers between devices with their start and end apart: 13 -> 10, of which waited for: 9 -> 5; matrix products, arithmetic and copies ran while one was open for 2% -> 1% of each run, Pallas kernels for 5% -> 3%
where the time goes in v5:
time: 174 us; the launch traced here: 172 us
  waiting for transfers between devices  98.3 us (56%)
  starting transfers between devices  36.1 us (21%)
  between operations  14.8 us (9%)
  Pallas kernels  12.3 us (7%)
  local copies, waits for them, and re-layouts  9.99 us (6%)
    ppermute x4, waiting for transfers between devices, to_previous(): return lax.ppermute(x, 'tm', [(i, i - 1) for i in range(1, count)])  46.4 us
    psum x1, waiting for transfers between devices, on_device(): tip_sum = lax.psum(term, 'tm')  43.7 us
    ppermute x4, starting transfers between devices, to_previous(): return lax.ppermute(x, 'tm', [(i, i - 1) for i in range(1, count)])  35.5 us
    unnamed x15, local copies, waits for them, and re-layouts  8.75 us
    ppermute x5, waiting for transfers between devices, swapped(): return lax.ppermute(x, 'space', [(0, 1), (1, 0)])  8.16 us
    pallas_call x1, Pallas kernels, eliminate(): pl.pallas_call(eliminate_kernel, out_shape=(jax.ShapeDtypeStruct(e.shape,...  4.36 us
  transfers between devices with their start and end apart: 10, of which 5 were waited for; matrix products, arithmetic and copies ran while one was open for 1% of the time, Pallas kernels for 3%

profile of v5, /device:TPU:2, one launch (start us, length us, event | category | flops | bytes accessed | tf_op | source)
XLA Modules:
  0.0 172.2 jit_solution(4447659558977498336)
XLA Ops:
  7.2 0.0 all-reduce.2.cloned.1.call-start
  7.2 0.1 collective-permute-start
  7.3 1.2 dynamic_slice.3
  9.2 0.6 add_convert_fusion.flags
  9.8 2.2 %collective-permute-done.other_d = bf16[1536,768]{1,0:T(8,128)(2,1)S(1)} collective-permute-done((bf16[1536,768]{1,0:T(8,128)(2,1)}, bf16[1536,768]{1,0:T(8,128)(2,1)S(1)}, u32[]{:S(2)}, u32[]{:S(2)}) %collective-permute-start) | collective-permute-done | bytes 2359328 | tf_op jit(solution)/shard_map/ppermute | solution.py:508
  12.0 1.4 copy-done.6
  13.4 4.4 %shard_map.85 = (bf16[1536,768]{1,0:T(8,128)(2,1)}, bf16[384,1536]{1,0:T(8,128)(2,1)}, bf16[384,384]{1,0:T(8,128)(2,1)}, bf16[400,384]{1,0:T(8,128)(2,1)}) custom-call(s32[3]{0:T(128)} %add_convert_fusion.flags, bf16[1536,768]{1,0:T(8,128)(2,1)} %own_d.1, bf16[1536,768]{1,0:T(8,128)(2,1)} %copy-done.6, bf16[1536,768]{1,0:T(8,128)(2,1)} %e_hbm.1, ...), custom_call_target="tpu_custom_call" | custom-call | flops 28000000000 | bytes 16777216 | tf_op jit(solution)/shard_map/pallas_call | solution.py:313
  17.8 0.2 collective-permute-start.3
  18.0 0.4 collective-permute-start.6
  18.4 5.9 %collective-permute-done.6.other_r = bf16[384,1536]{1,0:T(8,128)(2,1)S(1)} collective-permute-done((bf16[384,1536]{1,0:T(8,128)(2,1)}, bf16[384,1536]{1,0:T(8,128)(2,1)S(1)}, u32[]{:S(2)}, u32[]{:S(2)}) %collective-permute-start.6) | collective-permute-done | bytes 1179680 | tf_op jit(solution)/shard_map/ppermute | solution.py:508
  24.3 1.7 copy-done.4
  26.0 1.3 copy-done.5
  27.2 1.6 shard_map.88
  28.9 28.2 %collective-permute-start.7 = (bf16[768,768]{1,0:T(8,128)(2,1)}, bf16[768,768]{1,0:T(8,128)(2,1)}, u32[]{:S(2)}, u32[]{:S(2)}) collective-permute-start(bf16[768,768]{1,0:T(8,128)(2,1)} %shard_map.88), channel_id=1, source_target_pairs={{2,0},{4,2},{6,4},{8,6},{10,8},{12,10},{14,12},{3,1},{5,3},{7,5},{... | collective-permute-start | bytes 3538952 | tf_op jit(solution)/shard_map/ppermute | solution.py:513
  57.1 0.6 shard_map.86
  57.7 0.0 copy-start
  57.7 2.1 %collective-permute-start.4 = (bf16[384,768]{1,0:T(8,128)(2,1)S(1)}, bf16[384,768]{1,0:T(8,128)(2,1)S(1)}, u32[]{:S(2)}, u32[]{:S(2)}) collective-permute-start(bf16[384,768]{1,0:T(8,128)(2,1)S(1)} %shard_map.86), channel_id=1, source_target_pairs={{2,0},{4,2},{6,4},{8,6},{10,8},{12,10},{14,12},{3,1},{5,3},{7,5},{... | collective-permute-start | bytes 1769480 | tf_op jit(solution)/shard_map/ppermute | solution.py:513
  59.8 1.3 shard_map.89
  61.1 0.0 all-reduce.2.cloned.1.call-update
  61.1 36.5 %collective-permute-done.4.own_cross = bf16[384,768]{1,0:T(8,128)(2,1)S(1)} collective-permute-done((bf16[384,768]{1,0:T(8,128)(2,1)S(1)}, bf16[384,768]{1,0:T(8,128)(2,1)S(1)}, u32[]{:S(2)}, u32[]{:S(2)}) %collective-permute-start.4) | collective-permute-done | bytes 589856 | tf_op jit(solution)/shard_map/ppermute | solution.py:513
  97.6 0.0 collective-permute-start.5
  97.6 43.7 %all-reduce.2.cloned.1.call-done.own_sum = bf16[448,384]{1,0:T(8,128)(2,1)} async-done(((bf16[448,384]{1,0:T(8,128)(2,1)}), bf16[448,384]{1,0:T(8,128)(2,1)}) %all-reduce.2.cloned.1.call-update) | async-done | bytes 344080 | tf_op jit(solution)/shard_map/psum | solution.py:533
  141.3 3.3 %collective-permute-start.2 = (bf16[400,384]{1,0:T(8,128)(2,1)}, bf16[400,384]{1,0:T(8,128)(2,1)S(1)}, u32[]{:S(2)}, u32[]{:S(2)}) collective-permute-start(bf16[400,384]{1,0:T(8,128)(2,1)} %get-tuple-element.8), channel_id=1, source_target_pairs={{2,0},{4,2},{6,4},{8,6},{10,8},{12,10},{14,12},{3,1},{5,3},{7,5},{... | collective-permute-start | bytes 921608 | tf_op jit(solution)/shard_map/ppermute | solution.py:513
  144.6 1.9 %collective-permute-start.1 = (bf16[384,384]{1,0:T(8,128)(2,1)}, bf16[384,384]{1,0:T(8,128)(2,1)S(1)}, u32[]{:S(2)}, u32[]{:S(2)}) collective-permute-start(bf16[384,384]{1,0:T(8,128)(2,1)} %get-tuple-element.7), channel_id=1, source_target_pairs={{2,0},{4,2},{6,4},{8,6},{10,8},{12,10},{14,12},{3,1},{5,3},{7,5},{... | collective-permute-start | bytes 884744 | tf_op jit(solution)/shard_map/ppermute | solution.py:513
  146.5 0.0 collective-permute-done.8.other_sum
  146.5 0.0 copy-start.1
  146.6 1.1 copy-done.1
  147.6 1.0 copy-done.2
  148.6 1.8 %shard_map.90 = f32[768,384]{1,0:T(8,128)} custom-call(s32[3]{0:T(128)S(1)} %copy-done.3, bf16[768,384]{1,0:T(8,128)(2,1)S(1)} %copy-done.1, bf16[448,384]{1,0:T(8,128)(2,1)S(1)} %copy-done.2, bf16[448,384]{1,0:T(8,128)(2,1)S(1)} %collective-permute-done.8.other_sum), custom_call_target="tpu_custom_call" | custom-call | flops 1000000 | bytes 3145728 | tf_op jit(solution)/shard_map/pallas_call | solution.py:497
  150.4 9.9 %collective-permute-done.1.corner_in = bf16[384,384]{1,0:T(8,128)(2,1)S(1)} collective-permute-done((bf16[384,384]{1,0:T(8,128)(2,1)}, bf16[384,384]{1,0:T(8,128)(2,1)S(1)}, u32[]{:S(2)}, u32[]{:S(2)}) %collective-permute-start.1) | collective-permute-done | bytes 294944 | tf_op jit(solution)/shard_map/ppermute | solution.py:513
  160.3 2.6 %shard_map.87 = bf16[1536,768]{1,0:T(8,128)(2,1)} custom-call(s32[3]{0:T(128)S(1)} %copy-done.3, bf16[1536,768]{1,0:T(8,128)(2,1)S(1)} %copy-done, bf16[384,384]{1,0:T(8,128)(2,1)S(1)} %collective-permute-done.1.corner_in, bf16[400,384]{1,0:T(8,128)(2,1)S(1)} %collective-permute-done.2.folded, bf16[384,768]{1,0:T(8,128)(2,1)S(1)} %collective-permute-done.4.own_cross, ...), custom_call_target="tpu_custom_call" | custom-call | flops 1000000 | bytes 6291456 | tf_op jit(solution)/shard_map/pallas_call | solution.py:465
  163.0 2.4 %copy.11 = bf16[768,768]{1,0:T(8,128)(2,1)} copy(bf16[768,768]{1,0:T(8,128)(2,1)} %collective-permute-done.7) | data formatting | bytes 2359296
  (12 shorter events, 0.0 us)
Async XLA Ops:
  7.2 134.2 %all-reduce.2.cloned.1.call-start = ((), (), s32[]{:S(2)}) async-start(), calls=%async_computation | async-start | bytes 688128 | tf_op jit(solution)/shard_map/psum | solution.py:533
  7.2 4.8 %collective-permute-start = (bf16[1536,768]{1,0:T(8,128)(2,1)}, bf16[1536,768]{1,0:T(8,128)(2,1)S(1)}, u32[]{:S(2)}, u32[]{:S(2)}) collective-permute-start(bf16[1536,768]{1,0:T(8,128)(2,1)} %own_d.1), channel_id=1, source_target_pairs={{0,1},{1,0},{2,3},{3,2},{4,5},{5,4},{6,7},{7,6},{8,9},{9,8},{10,11... | collective-permute-start | bytes 7077896 | tf_op jit(solution)/shard_map/ppermute | solution.py:508
  9.8 14.5 %copy-start.3 = (s32[3]{0:T(128)S(1)}, s32[3]{0:T(128)}, u32[]{:S(2)}) copy-start(s32[3]{0:T(128)} %add_convert_fusion.flags) | copy-start | bytes 40
  12.0 1.4 copy-start.6
  17.8 39.3 %collective-permute-start.3 = (bf16[1536,768]{1,0:T(8,128)(2,1)}, bf16[1536,768]{1,0:T(8,128)(2,1)S(1)}, u32[]{:S(2)}, u32[]{:S(2)}) collective-permute-start(bf16[1536,768]{1,0:T(8,128)(2,1)} %get-tuple-element.9.own_e), channel_id=1, source_target_pairs={{0,1},{1,0},{2,3},{3,2},{4,5},{5,4},{6,7},{7,6},{8,9},{9,8},{10,11... | collective-permute-start | bytes 7077896 | tf_op jit(solution)/shard_map/ppermute | solution.py:508
  18.0 6.3 %collective-permute-start.6 = (bf16[384,1536]{1,0:T(8,128)(2,1)}, bf16[384,1536]{1,0:T(8,128)(2,1)S(1)}, u32[]{:S(2)}, u32[]{:S(2)}) collective-permute-start(bf16[384,1536]{1,0:T(8,128)(2,1)} %get-tuple-element.10.own_r), channel_id=1, source_target_pairs={{0,1},{1,0},{2,3},{3,2},{4,5},{5,4},{6,7},{7,6},{8,9},{9,8},{10,11... | collective-permute-start | bytes 3538952 | tf_op jit(solution)/shard_map/ppermute | solution.py:508
  24.3 1.7 copy-start.4
  26.0 1.3 copy-start.5
  28.9 121.5 %collective-permute-start.7 = (bf16[768,768]{1,0:T(8,128)(2,1)}, bf16[768,768]{1,0:T(8,128)(2,1)}, u32[]{:S(2)}, u32[]{:S(2)}) collective-permute-start(bf16[768,768]{1,0:T(8,128)(2,1)} %shard_map.88), channel_id=1, source_target_pairs={{2,0},{4,2},{6,4},{8,6},{10,8},{12,10},{14,12},{3,1},{5,3},{7,5},{... | collective-permute-start | bytes 3538952 | tf_op jit(solution)/shard_map/ppermute | solution.py:513
  57.7 102.6 %copy-start = (bf16[1536,768]{1,0:T(8,128)(2,1)S(1)}, bf16[1536,768]{1,0:T(8,128)(2,1)}, u32[]{:S(2)}) copy-start(bf16[1536,768]{1,0:T(8,128)(2,1)} %separator.1) | copy-start | bytes 7077892
  57.7 39.9 %collective-permute-start.4 = (bf16[384,768]{1,0:T(8,128)(2,1)S(1)}, bf16[384,768]{1,0:T(8,128)(2,1)S(1)}, u32[]{:S(2)}, u32[]{:S(2)}) collective-permute-start(bf16[384,768]{1,0:T(8,128)(2,1)S(1)} %shard_map.86), channel_id=1, source_target_pairs={{2,0},{4,2},{6,4},{8,6},{10,8},{12,10},{14,12},{3,1},{5,3},{7,5},{... | collective-permute-start | bytes 1769480 | tf_op jit(solution)/shard_map/ppermute | solution.py:513
  97.6 62.7 %collective-permute-start.5 = (bf16[384,768]{1,0:T(8,128)(2,1)S(1)}, bf16[384,768]{1,0:T(8,128)(2,1)S(1)}, u32[]{:S(2)}, u32[]{:S(2)}) collective-permute-start(bf16[384,768]{1,0:T(8,128)(2,1)S(1)} %collective-permute-done.4.own_cross), channel_id=1, source_target_pairs={{0,1},{1,0},{2,3},{3,2},{4,5},{5,4},{6,7},{7,6},{8,9},{9,8},{10,11... | collective-permute-start | bytes 1769480 | tf_op jit(solution)/shard_map/ppermute | solution.py:508
  141.3 5.2 %collective-permute-start.8 = (bf16[448,384]{1,0:T(8,128)(2,1)}, bf16[448,384]{1,0:T(8,128)(2,1)S(1)}, u32[]{:S(2)}, u32[]{:S(2)}) collective-permute-start(bf16[448,384]{1,0:T(8,128)(2,1)} %all-reduce.2.cloned.1.call-done.own_sum), channel_id=1, source_target_pairs={{0,1},{1,0},{2,3},{3,2},{4,5},{5,4},{6,7},{7,6},{8,9},{9,8},{10,11... | collective-permute-start | bytes 1032200 | tf_op jit(solution)/shard_map/ppermute | solution.py:508
  141.3 19.0 %collective-permute-start.2 = (bf16[400,384]{1,0:T(8,128)(2,1)}, bf16[400,384]{1,0:T(8,128)(2,1)S(1)}, u32[]{:S(2)}, u32[]{:S(2)}) collective-permute-start(bf16[400,384]{1,0:T(8,128)(2,1)} %get-tuple-element.8), channel_id=1, source_target_pairs={{2,0},{4,2},{6,4},{8,6},{10,8},{12,10},{14,12},{3,1},{5,3},{7,5},{... | collective-permute-start | bytes 921608 | tf_op jit(solution)/shard_map/ppermute | solution.py:513
  144.6 15.7 %collective-permute-start.1 = (bf16[384,384]{1,0:T(8,128)(2,1)}, bf16[384,384]{1,0:T(8,128)(2,1)S(1)}, u32[]{:S(2)}, u32[]{:S(2)}) collective-permute-start(bf16[384,384]{1,0:T(8,128)(2,1)} %get-tuple-element.7), channel_id=1, source_target_pairs={{2,0},{4,2},{6,4},{8,6},{10,8},{12,10},{14,12},{3,1},{5,3},{7,5},{... | collective-permute-start | bytes 884744 | tf_op jit(solution)/shard_map/ppermute | solution.py:513
  146.5 1.1 copy-start.1
  147.6 1.0 copy-start.2
Sparse Core Ops, SparseCore 0:
  61.3 80.0 all-reduce.1
